TPU v7x, 32 devices: a whole 2x2x4 slice. The times are simulated.
32 devices in a mesh: dp: 8 (over z, x), tensor: 4 (over y, core).
Axes of the slice: x: 2, y: 2, z: 4, core: 2. Of those that a mesh axis runs over, the one named last changes fastest.
Arguments:
- tokens: bfloat16 [16384, 1024], P(('dp', 'tensor')), may hold values from -6 to 6
- condition: bfloat16 [16, 1024], P('dp'), may hold values from -6 to 6
- ada_weight: bfloat16 [1024, 6144], P(None, 'tensor'), may hold values from -0.1875 to 0.1875
- ada_bias: bfloat16 [6144], P('tensor'), may hold values from -3 to 3
- qkv_weight: bfloat16 [1024, 3, 1024], P(None, None, 'tensor'), may hold values from -0.1875 to 0.1875
- qv_bias: bfloat16 [2, 1024], P(None, 'tensor'), may hold values from -3 to 3
- proj_weight: bfloat16 [1024, 1024], P('tensor'), may hold values from -0.75 to 0.75
- proj_bias: bfloat16 [1024], replicated, may hold values from -3 to 3
- up_weight: bfloat16 [4096, 1024], P('tensor'), may hold values from -0.1875 to 0.1875
- up_bias: bfloat16 [4096], P('tensor'), may hold values from -3 to 3
- down_weight: bfloat16 [4096, 1024], P('tensor'), may hold values from -0.09375 to 0.09375
- down_bias: bfloat16 [1024], replicated, may hold values from -3 to 3
- out_grad: bfloat16 [16384, 1024], P(('dp', 'tensor')), may hold values from -6 to 6
Outputs:
- block_out: bfloat16 [16384, 1024], P(('dp', 'tensor'))
- tokens_grad: float32 [16384, 1024], P(('dp', 'tensor'))
- condition_grad: float32 [16, 1024], P('dp')
- ada_weight_grad: float32 [1024, 6144], P(None, 'tensor')
- ada_bias_grad: float32 [6144], P('tensor')
- qkv_weight_grad: float32 [1024, 3, 1024], P(None, None, 'tensor')
- qv_bias_grad: float32 [2, 1024], P(None, 'tensor')
- proj_weight_grad: float32 [1024, 1024], P('tensor')
- proj_bias_grad: float32 [1024], replicated
- up_weight_grad: float32 [4096, 1024], P('tensor')
- up_bias_grad: float32 [4096], P('tensor')
- down_weight_grad: float32 [4096, 1024], P('tensor')
- down_bias_grad: float32 [1024], replicated
All inputs are finite; a program needn't handle non-finite values.
Results may differ from a plain program's by a relative error of at most 0.023.
The roundings to bfloat16 on the way count: a program that leaves them out, or rounds other values in their place, can miss the bound.
Values may be sent and summed in bfloat16 or wider, within the bound.
No kernel may reach another device: no remote copies, remote signals or barrier semaphores. Data moves between devices by JAX's collectives and lax.ppermute only.
A program may use at most 256 MiB of HBM per device.

v0:
```python
import math

import jax
import jax.numpy as jnp
from jax import lax
from jax.sharding import PartitionSpec as P

D = 1024
HD = 64
SEQ = 1024


norm_eps = 1e-06
highest = lax.Precision.HIGHEST


def layer_norm(values):
    row_mean = jnp.mean(values, axis=-1, keepdims=True)
    centered = values - row_mean
    inv_std = lax.rsqrt(jnp.mean(centered * centered, axis=-1, keepdims=True) + norm_eps)
    return (centered * inv_std, inv_std)


def norm_back(grad_normed, normed, inv_std):
    mean_grad = jnp.mean(grad_normed, axis=-1, keepdims=True)
    mean_cross = jnp.mean(grad_normed * normed, axis=-1, keepdims=True)
    return inv_std * (grad_normed - mean_grad - normed * mean_cross)


def gelu_tanh(values):
    return jax.nn.gelu(values, approximate=True)


def attend_query(inputs):
    query_rows, kv_rows = inputs
    key_rows = kv_rows[:, 0]
    value_rows = kv_rows[:, 1]
    score_scale = 1.0 / math.sqrt(HD)
    query_count = query_rows.shape[0]
    block_rows = min(512, query_count)
    out_parts = []
    lse_parts = []
    for start_row in range(0, query_count, block_rows):
        query_blk = query_rows[start_row : start_row + block_rows]
        scores = (
            jnp.einsum("qhd,khd->hqk", query_blk, key_rows, preferred_element_type=jnp.float32)
            * score_scale
        )
        row_max = jnp.max(scores, axis=-1, keepdims=True)
        exp_scores = jnp.exp(scores - row_max)
        row_total = jnp.sum(exp_scores, axis=-1, keepdims=True)
        probs_low = (exp_scores / row_total).astype(jnp.bfloat16)
        out_parts.append(
            jnp.einsum(
                "hqk,khd->qhd", probs_low, value_rows, preferred_element_type=jnp.float32
            ).astype(jnp.bfloat16)
        )
        lse_parts.append(row_max[..., 0] + jnp.log(row_total[..., 0]))
    return (jnp.concatenate(out_parts, axis=0), jnp.concatenate(lse_parts, axis=1))


def attend_query_back(inputs):
    query_rows, kv_rows, grad_rows, lse_rows = inputs
    key_rows = kv_rows[:, 0]
    value_rows = kv_rows[:, 1]
    score_scale = 1.0 / math.sqrt(HD)
    query_count = query_rows.shape[0]
    block_rows = min(512, query_count)
    key_grad = jnp.zeros(key_rows.shape, jnp.float32)
    value_grad = jnp.zeros(value_rows.shape, jnp.float32)
    query_parts = []
    for start_row in range(0, query_count, block_rows):
        query_blk = query_rows[start_row : start_row + block_rows]
        grad_blk = grad_rows[start_row : start_row + block_rows]
        scores = (
            jnp.einsum("qhd,khd->hqk", query_blk, key_rows, preferred_element_type=jnp.float32)
            * score_scale
        )
        probs = jnp.exp(scores - lse_rows[:, start_row : start_row + block_rows, None])
        probs_low = probs.astype(jnp.bfloat16)
        value_grad = value_grad + jnp.einsum(
            "hqk,qhd->khd", probs_low, grad_blk, preferred_element_type=jnp.float32
        )
        prob_grad = jnp.einsum(
            "qhd,khd->hqk", grad_blk, value_rows, preferred_element_type=jnp.float32
        )
        row_delta = jnp.sum(probs * prob_grad, axis=-1, keepdims=True)
        score_grad = (probs * (prob_grad - row_delta)).astype(jnp.bfloat16)
        query_parts.append(
            jnp.einsum("hqk,khd->qhd", score_grad, key_rows, preferred_element_type=jnp.float32)
            * score_scale
        )
        key_grad = (
            key_grad
            + jnp.einsum("hqk,qhd->khd", score_grad, query_blk, preferred_element_type=jnp.float32)
            * score_scale
        )
    query_grad = jnp.concatenate(query_parts, axis=0)
    return (query_grad, jnp.stack([key_grad, value_grad], axis=1))


def attend_latent(packed):
    out_rows, lse_rows = attend_query((packed[:, 0], packed[:, 1:]))
    return (out_rows, lse_rows)


def attend_back(inputs):
    packed, grad_lat, lse_lat = inputs
    query_grad, kv_grad = attend_query_back((packed[:, 0], packed[:, 1:], grad_lat, lse_lat))
    return jnp.concatenate([query_grad[:, None], kv_grad], axis=1).astype(jnp.bfloat16)


def shards(
    tokens,
    condition,
    ada_weight,
    ada_bias,
    qkv_weight,
    qv_bias,
    proj_weight,
    proj_bias,
    up_weight,
    up_bias,
    down_weight,
    down_bias,
    out_grad,
):
    rows_local = tokens.shape[0]
    latents_local = condition.shape[0]
    first_row = lax.axis_index("tensor") * rows_local
    row_latent = (first_row + jnp.arange(rows_local, dtype=jnp.int32)) // SEQ
    latent_pick = (
        row_latent[:, None] == jnp.arange(latents_local, dtype=jnp.int32)[None, :]
    ).astype(jnp.float32)
    cond_wide = condition.astype(jnp.float32)
    cond_sig = jax.nn.sigmoid(cond_wide)
    silu_low = (cond_wide * cond_sig).astype(jnp.bfloat16)
    mod_cols = (
        jnp.dot(silu_low, ada_weight, preferred_element_type=jnp.float32)
        + ada_bias.astype(jnp.float32)
    ).astype(jnp.bfloat16)
    mod_all = lax.all_gather(mod_cols, "tensor", axis=1, tiled=True).astype(jnp.float32)
    mod_rows = jnp.dot(latent_pick, mod_all, precision=highest)
    shift_attn, scale_attn, gate_attn, shift_mlp, scale_mlp, gate_mlp = [
        mod_rows[:, column_set * D : (column_set + 1) * D] for column_set in range(6)
    ]
    tokens_wide = tokens.astype(jnp.float32)
    normed_attn, inv_attn = layer_norm(tokens_wide)
    attn_input = (normed_attn * (1.0 + scale_attn) + shift_attn).astype(jnp.bfloat16)
    gathered_attn = lax.all_gather(attn_input, "tensor", axis=0, tiled=True)
    head_cols = qkv_weight.shape[2]
    heads_local = head_cols // HD
    qkv_flat = qkv_weight.reshape(D, 3 * head_cols)
    qkv_shift = jnp.concatenate([qv_bias[0], jnp.zeros_like(qv_bias[0]), qv_bias[1]]).astype(
        jnp.float32
    )
    qkv_rows = (
        jnp.dot(gathered_attn, qkv_flat, preferred_element_type=jnp.float32) + qkv_shift
    ).astype(jnp.bfloat16)
    latents_group = gathered_attn.shape[0] // SEQ
    qkv_packed = qkv_rows.reshape(latents_group, SEQ, 3, heads_local, HD)
    attn_heads, attn_lse = lax.map(attend_latent, qkv_packed)
    attn_flat = attn_heads.reshape(latents_group * SEQ, head_cols)
    proj_terms = jnp.dot(attn_flat, proj_weight, preferred_element_type=jnp.float32)
    branch_attn = lax.psum_scatter(
        proj_terms.astype(jnp.bfloat16), "tensor", scatter_dimension=0, tiled=True
    ).astype(jnp.float32) + proj_bias.astype(jnp.float32)
    hidden_state = tokens_wide + gate_attn * branch_attn
    normed_mlp, inv_mlp = layer_norm(hidden_state)
    mlp_input = (normed_mlp * (1.0 + scale_mlp) + shift_mlp).astype(jnp.bfloat16)
    gathered_mlp = lax.all_gather(mlp_input, "tensor", axis=0, tiled=True)
    pre_act = jnp.einsum(
        "rd,fd->rf", gathered_mlp, up_weight, preferred_element_type=jnp.float32
    ) + up_bias.astype(jnp.float32)
    hidden_low = gelu_tanh(pre_act).astype(jnp.bfloat16)
    down_terms = jnp.dot(hidden_low, down_weight, preferred_element_type=jnp.float32)
    branch_mlp = lax.psum_scatter(
        down_terms.astype(jnp.bfloat16), "tensor", scatter_dimension=0, tiled=True
    ).astype(jnp.float32) + down_bias.astype(jnp.float32)
    block_out = (hidden_state + gate_mlp * branch_mlp).astype(jnp.bfloat16)
    grad_wide = out_grad.astype(jnp.float32)
    grad_gate_mlp = grad_wide * branch_mlp
    grad_branch_mlp = (gate_mlp * grad_wide).astype(jnp.bfloat16)
    gathered_grad = lax.all_gather(grad_branch_mlp, "tensor", axis=0, tiled=True)
    grad_hidden = jnp.einsum(
        "rd,fd->rf", gathered_grad, down_weight, preferred_element_type=jnp.float32
    )
    grad_pre = jax.vjp(gelu_tanh, pre_act)[1](grad_hidden)[0].astype(jnp.bfloat16)
    down_weight_grad = jnp.einsum(
        "rf,rd->fd", hidden_low, gathered_grad, preferred_element_type=jnp.float32
    )
    up_weight_grad = jnp.einsum(
        "rf,rd->fd", grad_pre, gathered_mlp, preferred_element_type=jnp.float32
    )
    up_bias_grad = jnp.sum(grad_pre.astype(jnp.float32), axis=0)
    input_terms = jnp.dot(grad_pre, up_weight, preferred_element_type=jnp.float32)
    grad_mlp_input = lax.psum_scatter(
        input_terms.astype(jnp.bfloat16), "tensor", scatter_dimension=0, tiled=True
    ).astype(jnp.float32)
    grad_hidden_state = grad_wide + norm_back(
        grad_mlp_input * (1.0 + scale_mlp), normed_mlp, inv_mlp
    )
    grad_branch_attn = (gate_attn * grad_hidden_state).astype(jnp.bfloat16)
    gathered_back = lax.all_gather(grad_branch_attn, "tensor", axis=0, tiled=True)
    proj_weight_grad = jnp.einsum(
        "rc,rd->cd", attn_flat, gathered_back, preferred_element_type=jnp.float32
    )
    grad_attn_flat = jnp.einsum(
        "rd,cd->rc", gathered_back, proj_weight, preferred_element_type=jnp.float32
    ).astype(jnp.bfloat16)
    grad_heads = grad_attn_flat.reshape(latents_group, SEQ, heads_local, HD)
    grad_packed = lax.map(attend_back, (qkv_packed, grad_heads, attn_lse))
    grad_qkv = grad_packed.reshape(latents_group * SEQ, 3 * head_cols)
    qkv_weight_grad = jnp.einsum(
        "rd,rc->dc", gathered_attn, grad_qkv, preferred_element_type=jnp.float32
    ).reshape(qkv_weight.shape)
    bias_sums = jnp.sum(grad_qkv.astype(jnp.float32), axis=0).reshape(3, head_cols)
    qv_bias_grad = jnp.stack([bias_sums[0], bias_sums[2]])
    attn_terms = jnp.einsum("rc,dc->rd", grad_qkv, qkv_flat, preferred_element_type=jnp.float32)
    grad_attn_input = lax.psum_scatter(
        attn_terms.astype(jnp.bfloat16), "tensor", scatter_dimension=0, tiled=True
    ).astype(jnp.float32)
    tokens_grad = grad_hidden_state + norm_back(
        grad_attn_input * (1.0 + scale_attn), normed_attn, inv_attn
    )
    grad_mod_rows = jnp.concatenate(
        [
            grad_attn_input,
            grad_attn_input * normed_attn,
            grad_hidden_state * branch_attn,
            grad_mlp_input,
            grad_mlp_input * normed_mlp,
            grad_gate_mlp,
        ],
        axis=1,
    )
    grad_mod_local = jnp.dot(latent_pick.T, grad_mod_rows, precision=highest)
    grad_mod_cols = lax.psum_scatter(
        grad_mod_local.astype(jnp.bfloat16), "tensor", scatter_dimension=1, tiled=True
    )
    ada_weight_grad = jnp.dot(silu_low.T, grad_mod_cols, preferred_element_type=jnp.float32)
    ada_bias_grad = jnp.sum(grad_mod_cols.astype(jnp.float32), axis=0)
    silu_part = jnp.dot(grad_mod_cols, ada_weight.T, preferred_element_type=jnp.float32)
    proj_bias_part = jnp.sum(grad_branch_attn.astype(jnp.float32), axis=0)
    down_bias_part = jnp.sum(grad_branch_mlp.astype(jnp.float32), axis=0)
    silu_grad, proj_bias_grad, down_bias_grad = (
        lax.psum(silu_part.astype(jnp.bfloat16), "tensor").astype(jnp.float32),
        lax.psum(proj_bias_part.astype(jnp.bfloat16), "tensor").astype(jnp.float32),
        lax.psum(down_bias_part.astype(jnp.bfloat16), "tensor").astype(jnp.float32),
    )
    condition_grad = silu_grad * (cond_sig * (1.0 + cond_wide * (1.0 - cond_sig)))
    summed = (
        lax.psum(ada_weight_grad.astype(jnp.bfloat16), "dp").astype(jnp.float32),
        lax.psum(ada_bias_grad.astype(jnp.bfloat16), "dp").astype(jnp.float32),
        lax.psum(qkv_weight_grad.astype(jnp.bfloat16), "dp").astype(jnp.float32),
        lax.psum(qv_bias_grad.astype(jnp.bfloat16), "dp").astype(jnp.float32),
        lax.psum(proj_weight_grad.astype(jnp.bfloat16), "dp").astype(jnp.float32),
        lax.psum(proj_bias_grad.astype(jnp.bfloat16), "dp").astype(jnp.float32),
        lax.psum(up_weight_grad.astype(jnp.bfloat16), "dp").astype(jnp.float32),
        lax.psum(up_bias_grad.astype(jnp.bfloat16), "dp").astype(jnp.float32),
        lax.psum(down_weight_grad.astype(jnp.bfloat16), "dp").astype(jnp.float32),
        lax.psum(down_bias_grad.astype(jnp.bfloat16), "dp").astype(jnp.float32),
    )
    return (block_out, tokens_grad, condition_grad) + tuple(summed)


def solution(mesh):
    placed = (
        P(("dp", "tensor"), None),
        P("dp", None),
        P(None, "tensor"),
        P("tensor"),
        P(None, None, "tensor"),
        P(None, "tensor"),
        P("tensor", None),
        P(),
        P("tensor", None),
        P("tensor"),
        P("tensor", None),
        P(),
        P(("dp", "tensor"), None),
    )
    return jax.shard_map(
        shards,
        mesh=mesh,
        in_specs=placed,
        out_specs=(
            P(("dp", "tensor"), None),
            P(("dp", "tensor"), None),
            P("dp", None),
            P(None, "tensor"),
            P("tensor"),
            P(None, None, "tensor"),
            P(None, "tensor"),
            P("tensor", None),
            P(),
            P("tensor", None),
            P("tensor"),
            P("tensor", None),
            P(),
        ),
        check_vma=False,
    )
```

profile of v0, /device:TPU:0, one launch (start us, length us, event | category | flops | bytes accessed | tf_op | source)
XLA Modules:
  0.0 895.1 jit_solution(1262495356426923019)
XLA Ops:
  12.4 6.3 all_gather.15
  29.5 33.4 %all-gather.5.cloned.1.call-done = bf16[2048,1024]{1,0:T(8,128)(2,1)} async-done(((bf16[512,1024]{1,0:T(8,128)(2,1)}), bf16[2048,1024]{1,0:T(8,128)(2,1)}) %all-gather.5.cloned.1.call-update) | async-done | bytes 4194320 | tf_op jit(solution)/shard_map/all_gather | solution.py:150
  62.9 7.8 add_convert_fusion
  70.7 10.1 %reshape.206 = bf16[2,1024,3,4,64]{4,3,2,1,0:T(4,128)(2,1)} reshape(bf16[2048,768]{1,0:T(8,128)(2,1)} %add_convert_fusion) | data formatting | bytes 6291456 | tf_op jit(solution)/shard_map/reshape | solution.py:161
  80.8 9.8 %copy.41 = bf16[2,1024,3,4,64]{1,4,3,2,0:T(8,128)(2,1)} copy(bf16[2,1024,3,4,64]{4,3,2,1,0:T(4,128)(2,1)} %reshape.206) | data formatting | bytes 6291456 | tf_op jit(solution)/shard_map/while | solution.py:162
  90.6 27.8 %while.22 = (s32[]{:T(128)}, bf16[2,1024,4,64]{1,3,2,0:T(8,128)(2,1)}, f32[2,4,1024]{2,1,0:T(4,128)S(1)}, bf16[2,1024,3,4,64]{1,4,3,2,0:T(8,128)(2,1)}, s32[]{:T(128)}) while((s32[]{:T(128)}, bf16[2,1024,4,64]{1,3,2,0:T(8,128)(2,1)}, f32[2,4,1024]{2,1,0:T(4,128)S(1)}, bf16[2,1024,3,4,64]{1,4,3,2,0:T(8,128)(2,1)}, s32[]{:T(128)}) %tuple.75), condition=%wide.region_7.8_spmd, body=%wide.region_2.7_spmd.sunk | while | flops 1112801280 | bytes 66224264 | solution.py:162
  126.1 44.1 %reduce-scatter.8.cloned.1.call-done = bf16[512,1024]{1,0:T(8,128)(2,1)} async-done(((bf16[2048,1024]{1,0:T(8,128)(2,1)}), bf16[512,1024]{1,0:T(8,128)(2,1)}) %reduce-scatter.8.cloned.1.call-update) | async-done | bytes 1048592 | tf_op jit(solution)/shard_map/reduce_scatter | solution.py:165
  181.8 30.6 %all-gather.7.cloned.1.call-done = bf16[2048,1024]{1,0:T(8,128)(2,1)} async-done(((bf16[512,1024]{1,0:T(8,128)(2,1)}), bf16[2048,1024]{1,0:T(8,128)(2,1)}) %all-gather.7.cloned.1.call-update) | async-done | bytes 4194320 | tf_op jit(solution)/shard_map/all_gather | solution.py:171
  212.4 7.1 fusion.110
  223.5 6.9 convolution_convert_fusion.5
  230.6 18.4 %all-gather.9.cloned.1.call-done = bf16[2048,1024]{1,0:T(8,128)(2,1)} async-done(((bf16[512,1024]{1,0:T(8,128)(2,1)}), bf16[2048,1024]{1,0:T(8,128)(2,1)}) %all-gather.9.cloned.1.call-update) | async-done | bytes 4194320 | tf_op jit(solution)/shard_map/all_gather | solution.py:184
  248.9 14.8 %fusion.102 = (bf16[1024]{0:T(1024)(128)(2,1)}, bf16[2048,1024]{1,0:T(8,128)(2,1)S(1)}) fusion(f32[2048,1024]{1,0:T(8,128)} %copy-done.57, f32[1024]{0:T(1024)S(1)} %convert_element_type.208, bf16[2048,1024]{1,0:T(8,128)(2,1)} %all-gather.9.cloned.1.call-done, bf16[1024,1024]{1,0:T(8,128)(2,1)} %param.27), kind=kOutput, calls=%fused_computation.184 | convolution fusion | flops 4341103616 | bytes 18880512 | tf_op jit(solution)/shard_map/rd,fd->rf/dot_general | solution.py:185
  265.8 6.0 convolution_convert_fusion.4
  272.4 24.0 %reduce-scatter.10.cloned.1.call-done = bf16[512,1024]{1,0:T(8,128)(2,1)} async-done(((bf16[2048,1024]{1,0:T(8,128)(2,1)}), bf16[512,1024]{1,0:T(8,128)(2,1)}) %reduce-scatter.10.cloned.1.call-update) | async-done | bytes 1048592 | tf_op jit(solution)/shard_map/reduce_scatter | solution.py:177
  296.5 47.6 %reduce-scatter.12.cloned.1.call-done = bf16[512,1024]{1,0:T(8,128)(2,1)} async-done(((bf16[2048,1024]{1,0:T(8,128)(2,1)}), bf16[512,1024]{1,0:T(8,128)(2,1)}) %reduce-scatter.12.cloned.1.call-update) | async-done | bytes 1048592 | tf_op jit(solution)/shard_map/reduce_scatter | solution.py:197
  344.0 5.4 fusion.83
  354.1 34.6 %all-gather.11.cloned.1.call-done = bf16[2048,1024]{1,0:T(8,128)(2,1)} async-done(((bf16[512,1024]{1,0:T(8,128)(2,1)}), bf16[2048,1024]{1,0:T(8,128)(2,1)}) %all-gather.11.cloned.1.call-update) | async-done | bytes 4194320 | tf_op jit(solution)/shard_map/all_gather | solution.py:204
  401.7 64.4 %while.23 = (s32[]{:T(128)}, bf16[2,1024,3,4,64]{1,4,3,2,0:T(8,128)(2,1)}, bf16[2,1024,3,4,64]{1,4,3,2,0:T(8,128)(2,1)}, f32[2,4,1024]{2,1,0:T(4,128)S(1)}, bf16...) while((s32[]{:T(128)}, bf16[2,1024,3,4,64]{1,4,3,2,0:T(8,128)(2,1)}, ...), condition=%wide.region_18.19_spmd, body=%wide.region_15.18_spmd.sunk | while | flops 2742284288 | bytes 173686992 | solution.py:212
  414.2 4.6 multiply_reduce_fusion.13
  418.8 8.1 multiply_convert_fusion.8
  450.8 8.1 multiply_convert_fusion.8
  466.1 5.1 copy.46
  474.0 5.0 convolution_convert_fusion.3
  479.5 9.5 %convolution_convert_fusion.8 = bf16[1024,1024]{1,0:T(8,128)(2,1)} fusion(bf16[2048,1024]{1,0:T(8,128)(2,1)} %copy-done.56, bf16[2048,1024]{1,0:T(8,128)(2,1)} %all-gather.7.cloned.1.call-done), kind=kOutput, calls=%fused_computation.140 | convolution fusion | flops 4296015872 | bytes 10485760 | tf_op jit(solution)/shard_map/rf,rd->fd/dot_general | solution.py:192
  489.0 11.2 %convolution_convert_fusion.7 = bf16[1024,1024]{1,0:T(8,128)(2,1)} fusion(bf16[2048,1024]{1,0:T(8,128)(2,1)S(1)} %copy-done.53, f32[2048,1024]{1,0:T(8,128)} %copy-done.57, f32[1024]{0:T(1024)S(1)} %copy-done.47), kind=kOutput, calls=%fused_computation.139 | convolution fusion | flops 4316987392 | bytes 14684160 | tf_op jit(solution)/shard_map/rf,rd->fd/dot_general | solution.py:189
  500.3 5.0 fusion.78
  505.3 18.5 %reduce-scatter.14.cloned.1.call-done = bf16[512,1024]{1,0:T(8,128)(2,1)} async-done(((bf16[2048,1024]{1,0:T(8,128)(2,1)}), bf16[512,1024]{1,0:T(8,128)(2,1)}) %reduce-scatter.14.cloned.1.call-update) | async-done | bytes 1048592 | tf_op jit(solution)/shard_map/reduce_scatter | solution.py:220
  545.8 23.4 %reduce-scatter.16.cloned.1.call-done = bf16[1536,2]{1,0:T(8,128)(2,1)} async-done(((bf16[6144,2]{1,0:T(8,128)(2,1)}), bf16[1536,2]{1,0:T(8,128)(2,1)}) %reduce-scatter.16.cloned.1.call-update) | async-done | bytes 6160
  580.1 6.8 all-reduce.2
  587.1 39.7 %all-reduce = (bf16[1536]{0:T(1024)(128)(2,1)S(1)}, bf16[2,256]{1,0:T(2,128)(2,1)S(1)}, bf16[1024]{0:T(1024)(128)(2,1)S(1)}, bf16[1024]{0:T(1024)(128)(2,1)S(1)}, bf16[1024]{0:T(1024)(128)(2,1)S(1)}) all-reduce(bf16[1536]{0:T(1024)(128)(2,1)S(1)} %bitcast_reduce_fusion, ...), channel_id=1, replica_groups=mesh['dp'=8,'tensor'=4] {'dp'}, use_global_device_ids=true, to_apply=%region_26.27 | all-reduce | flops 5120 | bytes 20480 | tf_op jit(solution)/shard_map/psum | solution.py:254
  631.0 241.9 %all-reduce.5.cloned.1.call-done = (bf16[1024,1536]{1,0:T(8,128)(2,1)}, bf16[1024,3,256]{2,0,1:T(8,128)(2,1)}, bf16[256,1024]{1,0:T(8,128)(2,1)}, bf16[1024,1024]{1,0:T(8,128)(2,1)}, bf16[1024,1024]{1,0:T(8,128)(2,1)}) async-done(((bf16[1024,1536]{1,0:T(8,128)(2,1)}, bf16[1024,3,256]{2,0,1:T(8,128)(2,1)}, bf16[256,1024]{1,0:T(8,128)(2,1)}, bf16[1024,1024]{1,0:T(8,128)(2,1)}, bf16[1024,1024]{1,0:T(8,128)(2,1)}), ...) | async-done | bytes 9437200 | tf_op jit(solution)/shard_map/psum | solution.py:253
  875.1 5.6 convert_element_type.227
  (258 shorter events, 179.8 us)
Async XLA Ops:
  7.2 55.7 %all-gather.5.cloned.1.call-start = ((), (), s32[]{:S(2)}) async-start(), calls=%async_computation.5 | async-start | bytes 5242880 | tf_op jit(solution)/shard_map/all_gather | solution.py:150
  7.3 11.4 %copy-start.29 = (s32[512]{0:T(512)}, s32[512]{0:T(512)S(1)}, u32[]{:S(2)}) copy-start(s32[512]{0:T(512)S(1)} %add_select_fusion) | copy-start | bytes 6148
  8.9 11.7 %copy-start.33 = (f32[512]{0:T(512)}, f32[512]{0:T(512)S(1)}, u32[]{:S(2)}) copy-start(f32[512]{0:T(512)S(1)} %broadcast_multiply_fusion.5) | copy-start | bytes 6148
  10.5 10.0 %copy-start.42 = (f32[512]{0:T(512)}, f32[512]{0:T(512)S(1)}, u32[]{:S(2)}) copy-start(f32[512]{0:T(512)S(1)} %add_rsqrt_fusion.1) | copy-start | bytes 6148
  18.7 6.4 copy-start.6
  26.6 143.6 %reduce-scatter.8.cloned.1.call-start = ((), (), s32[]{:S(2)}) async-start(), calls=%async_computation.6 | async-start | bytes 5242880 | tf_op jit(solution)/shard_map/reduce_scatter | solution.py:165
  125.4 87.0 %all-gather.7.cloned.1.call-start = ((), (), s32[]{:S(2)}) async-start(), calls=%async_computation.7 | async-start | bytes 5242880 | tf_op jit(solution)/shard_map/all_gather | solution.py:171
  126.1 46.8 %copy-start.39 = (f32[1024]{0:T(1024)}, f32[1024]{0:T(1024)S(1)}, u32[]{:S(2)}) copy-start(f32[1024]{0:T(1024)S(1)} %convert_element_type.206) | copy-start | bytes 12292
  172.9 176.6 %copy-start.31 = (f32[512]{0:T(512)}, f32[512]{0:T(512)S(1)}, u32[]{:S(2)}) copy-start(f32[512]{0:T(512)S(1)} %broadcast_multiply_fusion.4) | copy-start | bytes 6148
  174.1 175.3 %copy-start.35 = (f32[512]{0:T(512)}, f32[512]{0:T(512)S(1)}, u32[]{:S(2)}) copy-start(f32[512]{0:T(512)S(1)} %add_rsqrt_fusion) | copy-start | bytes 6148
  177.8 71.1 %all-gather.9.cloned.1.call-start = ((), (), s32[]{:S(2)}) async-start(), calls=%async_computation.9 | async-start | bytes 5242880 | tf_op jit(solution)/shard_map/all_gather | solution.py:184
  181.7 114.7 %reduce-scatter.10.cloned.1.call-start = ((), (), s32[]{:S(2)}) async-start(), calls=%async_computation.8 | async-start | bytes 5242880 | tf_op jit(solution)/shard_map/reduce_scatter | solution.py:177
  181.8 67.1 %copy-start.46 = (f32[1024]{0:T(1024)}, f32[1024]{0:T(1024)S(1)}, u32[]{:S(2)}) copy-start(f32[1024]{0:T(1024)S(1)} %convert_element_type.208) | copy-start | bytes 12292
  212.4 11.1 %copy-start.54 = (bf16[1024,1024]{1,0:T(8,128)(2,1)S(1)}, bf16[1024,1024]{1,0:T(8,128)(2,1)}, u32[]{:S(2)}) copy-start(bf16[1024,1024]{1,0:T(8,128)(2,1)} %param.27) | copy-start | bytes 6291460
  230.5 113.5 %reduce-scatter.12.cloned.1.call-start = ((), (), s32[]{:S(2)}) async-start(), calls=%async_computation.10 | async-start | bytes 5242880 | tf_op jit(solution)/shard_map/reduce_scatter | solution.py:197
  248.9 16.8 %copy-start.55 = (bf16[1024,1024]{1,0:T(8,128)(2,1)S(1)}, bf16[1024,1024]{1,0:T(8,128)(2,1)}, u32[]{:S(2)}) copy-start(bf16[1024,1024]{1,0:T(8,128)(2,1)} %param.25) | copy-start | bytes 6291460
  271.8 116.9 %all-gather.11.cloned.1.call-start = ((), (), s32[]{:S(2)}) async-start(), calls=%async_computation.11 | async-start | bytes 5242880 | tf_op jit(solution)/shard_map/all_gather | solution.py:204
  272.4 77.0 %copy-start.37 = (f32[1024]{0:T(1024)}, f32[1024]{0:T(1024)S(1)}, u32[]{:S(2)}) copy-start(f32[1024]{0:T(1024)S(1)} %convert_element_type.212) | copy-start | bytes 12292
  354.0 169.7 %reduce-scatter.14.cloned.1.call-start = ((), (), s32[]{:S(2)}) async-start(), calls=%async_computation.12 | async-start | bytes 5242880 | tf_op jit(solution)/shard_map/reduce_scatter | solution.py:220
  479.0 10.0 %copy-start.47 = (f32[1024]{0:T(1024)S(1)}, f32[1024]{0:T(1024)}, u32[]{:S(2)}) copy-start(f32[1024]{0:T(1024)} %copy-done.46) | copy-start | bytes 12292
  479.0 90.1 %reduce-scatter.16.cloned.1.call-start = ((), (), s32[]{:S(2)}) async-start(), calls=%async_computation.13 | async-start | bytes 1966080
  479.5 9.5 %copy-start.53 = (bf16[2048,1024]{1,0:T(8,128)(2,1)S(1)}, bf16[2048,1024]{1,0:T(8,128)(2,1)}, u32[]{:S(2)}) copy-start(bf16[2048,1024]{1,0:T(8,128)(2,1)} %all-gather.9.cloned.1.call-done) | copy-start | bytes 12582916
  489.0 11.2 %copy-start.21 = (bf16[96,8,2,1024]{3,1,2,0:T(8,128)(2,1)S(1)}, bf16[96,8,2,1024]{3,1,2,0:T(8,128)(2,1)}, u32[]{:S(2)}) copy-start(bf16[96,8,2,1024]{3,1,2,0:T(8,128)(2,1)} %copy-done.20) | copy-start | bytes 9437188
  489.0 11.2 %copy-start.52 = (bf16[2048,1024]{1,0:T(8,128)(2,1)S(1)}, bf16[2048,1024]{1,0:T(8,128)(2,1)}, u32[]{:S(2)}) copy-start(bf16[2048,1024]{1,0:T(8,128)(2,1)} %all-gather.5.cloned.1.call-done) | copy-start | bytes 12582916
  500.3 25.1 %copy-start.34 = (f32[512]{0:T(512)S(1)}, f32[512]{0:T(512)}, u32[]{:S(2)}) copy-start(f32[512]{0:T(512)} %copy-done.33) | copy-start | bytes 6148
  500.3 25.1 %copy-start.43 = (f32[512]{0:T(512)S(1)}, f32[512]{0:T(512)}, u32[]{:S(2)}) copy-start(f32[512]{0:T(512)} %copy-done.42) | copy-start | bytes 6148
  505.3 23.6 %copy-start.40 = (f32[1024]{0:T(1024)S(1)}, f32[1024]{0:T(1024)}, u32[]{:S(2)}) copy-start(f32[1024]{0:T(1024)} %copy-done.39) | copy-start | bytes 12292
  540.9 28.2 %copy-start.41 = (bf16[2,1024]{1,0:T(2,128)(2,1)S(1)}, bf16[2,1024]{1,0:T(2,128)(2,1)}, u32[]{:S(2)}) copy-start(bf16[2,1024]{1,0:T(2,128)(2,1)} %param.18) | copy-start | bytes 12292
  541.0 332.0 %all-reduce.5.cloned.1.call-start = ((), (), s32[]{:S(2)}) async-start(), calls=%async_computation.14 | async-start | bytes 18874368 | tf_op jit(solution)/shard_map/psum | solution.py:253
  572.9 6.4 copy-start.19
  572.9 7.3 copy-start.44
  572.9 7.2 copy-start.45
  (41 other events, 119.0 us)
Sparse Core Ops, SparseCore 0:
  26.7 36.1 all-gather.4
  125.5 44.5 reduce-scatter.7
  177.9 34.4 all-gather.6
  214.4 34.4 all-gather.8
  251.9 44.5 reduce-scatter.9
  299.4 44.5 reduce-scatter.11
  354.2 34.4 all-gather.10
  479.1 44.5 reduce-scatter.13
  541.1 28.0 reduce-scatter.15
  574.3 298.5 all-reduce.4
where the time goes:
time: 900 us; the launch traced here: 895 us
  waiting for transfers between devices  517 us (57%)
  matrix products  153 us (17%)
  other arithmetic  82.5 us (9%)
  local copies, waits for them, and re-layouts  73.8 us (8%)
  blocking collectives  52.7 us (6%)
  between operations  15 us (2%)
    psum x1, waiting for transfers between devices, shards(): lax.psum(ada_weight_grad.astype(jnp.bfloat16), 'dp').astype(jnp.float32)  242 us
    reduce_scatter x1, waiting for transfers between devices, shards(): lax.psum_scatter(input_terms.astype(jnp.bfloat16), 'tensor', scatter_dime...  47.6 us
    reduce_scatter x1, waiting for transfers between devices, shards(): lax.psum_scatter(proj_terms.astype(jnp.bfloat16), 'tensor', scatter_dimen...  44.1 us
    psum x1, blocking collectives, shards(): lax.psum(ada_bias_grad.astype(jnp.bfloat16), 'dp').astype(jnp.float32)  39.7 us
    all_gather x1, waiting for transfers between devices, shards(): lax.all_gather(grad_branch_attn, 'tensor', axis=0, tiled=True)  34.6 us
    all_gather x1, waiting for transfers between devices, shards(): gathered_attn = lax.all_gather(attn_input, 'tensor', axis=0, tiled=True)  33.4 us
    all_gather x1, waiting for transfers between devices, shards(): gathered_mlp = lax.all_gather(mlp_input, 'tensor', axis=0, tiled=True)  30.6 us
    reduce_scatter x1, waiting for transfers between devices, shards(): lax.psum_scatter(down_terms.astype(jnp.bfloat16), 'tensor', scatter_dimen...  24 us
  transfers between devices with their start and end apart: 10, of which 10 were waited for; matrix products, arithmetic and copies ran while one was open for 9% of the time, Pallas kernels for 0%

commit v1 on v0

v1 whole, which is shorter than its diff:
```python
import functools
import math

import jax
import jax.numpy as jnp
from jax import lax
from jax.experimental import pallas as pl
from jax.experimental.pallas import tpu as pltpu
from jax.sharding import PartitionSpec as P

D = 1024
HD = 64
SEQ = 1024
LANES = 128

norm_eps = 1e-06
score_scale = 1.0 / math.sqrt(HD)
query_block = 512
vmem_limit = 56 * 1024 * 1024


def layer_norm(values):
    row_mean = jnp.mean(values, axis=-1, keepdims=True)
    centered = values - row_mean
    inv_std = lax.rsqrt(jnp.mean(centered * centered, axis=-1, keepdims=True) + norm_eps)
    return (centered * inv_std, inv_std)


def norm_back(grad_normed, normed, inv_std):
    mean_grad = jnp.mean(grad_normed, axis=-1, keepdims=True)
    mean_cross = jnp.mean(grad_normed * normed, axis=-1, keepdims=True)
    return inv_std * (grad_normed - mean_grad - normed * mean_cross)


def gelu_tanh(values):
    return jax.nn.gelu(values, approximate=True)


def contract(left, right, left_dim, right_dim):
    return lax.dot_general(
        left, right, (((left_dim,), (right_dim,)), ((), ())), preferred_element_type=jnp.float32
    )


def head_mask(shape, head):
    lane = lax.broadcasted_iota(jnp.int32, shape, 1)
    return (lane >= head * HD) & (lane < (head + 1) * HD)


def attend_kernel(q_ref, k_ref, v_ref, out_ref, lse_ref):
    heads = LANES // HD
    keys = k_ref[...]
    values = v_ref[...]
    masks = [head_mask(keys.shape, head) for head in range(heads)]
    zero = jnp.zeros_like(keys)
    keys_of = [jnp.where(mask, keys, zero) for mask in masks]
    values_of = [jnp.where(mask, values, zero) for mask in masks]
    for start in range(0, SEQ, query_block):
        rows = pl.ds(start, query_block)
        query = q_ref[rows, :] * jnp.bfloat16(score_scale)
        total = None
        for head in range(heads):
            scores = contract(keys_of[head], query, 1, 1)
            top = jnp.max(scores, axis=0, keepdims=True)
            weights = jnp.exp(scores - top)
            norm = jnp.sum(weights, axis=0, keepdims=True)
            probs = (weights * (1.0 / norm)).astype(jnp.bfloat16)
            part = contract(probs, values_of[head], 0, 0)
            total = part if total is None else total + part
            lse_ref[0, head : head + 1, rows] = top + jnp.log(norm)
        out_ref[rows, :] = total.astype(jnp.bfloat16)


def attend_back_kernel(
    q_ref, k_ref, v_ref, do_ref, lse_ref, dq_ref, dk_ref, dv_ref, dk_acc, dv_acc
):
    heads = LANES // HD
    keys = k_ref[...]
    values = v_ref[...]
    mask_keys = [head_mask(keys.shape, head) for head in range(heads)]
    zero = jnp.zeros_like(keys)
    keys_of = [jnp.where(mask, keys, zero) for mask in mask_keys]
    values_of = [jnp.where(mask, values, zero) for mask in mask_keys]
    for start in range(0, SEQ, query_block):
        rows = pl.ds(start, query_block)
        query = q_ref[rows, :] * jnp.bfloat16(score_scale)
        grad = do_ref[rows, :]
        mask_query = [head_mask(query.shape, head) for head in range(heads)]
        none = jnp.zeros_like(query)
        total = None
        dk_new = None
        dv_new = None
        for head in range(heads):
            scores = contract(keys_of[head], query, 1, 1)
            probs = jnp.exp(scores - lse_ref[0, head : head + 1, rows])
            prob_grad = contract(values_of[head], grad, 1, 1)
            delta = jnp.sum(probs * prob_grad, axis=0, keepdims=True)
            score_grad = (probs * (prob_grad - delta)).astype(jnp.bfloat16)
            dv_part = contract(
                probs.astype(jnp.bfloat16), jnp.where(mask_query[head], grad, none), 1, 0
            )
            dk_part = contract(score_grad, jnp.where(mask_query[head], query, none), 1, 0)
            dq_part = contract(score_grad, keys_of[head], 0, 0)
            dv_new = dv_part if dv_new is None else dv_new + dv_part
            dk_new = dk_part if dk_new is None else dk_new + dk_part
            total = dq_part if total is None else total + dq_part
        dq_ref[rows, :] = (total * score_scale).astype(jnp.bfloat16)
        if start == 0:
            dk_acc[...] = dk_new
            dv_acc[...] = dv_new
        else:
            dk_acc[...] += dk_new
            dv_acc[...] += dv_new
    dk_ref[...] = dk_acc[...].astype(jnp.bfloat16)
    dv_ref[...] = dv_acc[...].astype(jnp.bfloat16)


def column_spec(offset):
    return pl.BlockSpec((SEQ, LANES), lambda step: (0, step + offset))


def attend(qkv_rows, head_cols):
    blocks = head_cols // LANES
    lse_spec = pl.BlockSpec((1, LANES // HD, SEQ), lambda step: (step, 0, 0))
    return pl.pallas_call(
        attend_kernel,
        grid=(blocks,),
        in_specs=[column_spec(0), column_spec(blocks), column_spec(2 * blocks)],
        out_specs=[column_spec(0), lse_spec],
        out_shape=[
            jax.ShapeDtypeStruct((SEQ, head_cols), jnp.bfloat16),
            jax.ShapeDtypeStruct((blocks, LANES // HD, SEQ), jnp.float32),
        ],
        compiler_params=pltpu.CompilerParams(vmem_limit_bytes=vmem_limit),
        name="attend",
    )(qkv_rows, qkv_rows, qkv_rows)


def attend_back(qkv_rows, grad_heads, lse, head_cols):
    blocks = head_cols // LANES
    lse_spec = pl.BlockSpec((1, LANES // HD, SEQ), lambda step: (step, 0, 0))
    part = jax.ShapeDtypeStruct((SEQ, head_cols), jnp.bfloat16)
    return pl.pallas_call(
        attend_back_kernel,
        grid=(blocks,),
        in_specs=[
            column_spec(0),
            column_spec(blocks),
            column_spec(2 * blocks),
            column_spec(0),
            lse_spec,
        ],
        out_specs=[column_spec(0)] * 3,
        out_shape=[part] * 3,
        scratch_shapes=[pltpu.VMEM((SEQ, LANES), jnp.float32)] * 2,
        compiler_params=pltpu.CompilerParams(vmem_limit_bytes=vmem_limit),
        name="attend_back",
    )(qkv_rows, qkv_rows, qkv_rows, grad_heads, lse)


def shards(
    dp_size,
    tensor_size,
    tokens,
    condition,
    ada_weight,
    ada_bias,
    qkv_weight,
    qv_bias,
    proj_weight,
    proj_bias,
    up_weight,
    up_bias,
    down_weight,
    down_bias,
    out_grad,
):
    rows_local = tokens.shape[0]
    pair = SEQ // rows_local
    groups = tensor_size // pair
    latents_local = condition.shape[0]
    tensor_at = lax.axis_index("tensor")
    dp_at = lax.axis_index("dp")
    f32 = jnp.float32
    bf16 = jnp.bfloat16

    def pair_move(values, step):
        moves = [(i, i // pair * pair + (i + step) % pair) for i in range(tensor_size)]
        return lax.ppermute(values, "tensor", moves)

    def group_move(values, step):
        moves = [(i, (i + step * pair) % tensor_size) for i in range(tensor_size)]
        return lax.ppermute(values, "tensor", moves)

    def pair_gather(rows):
        return jnp.concatenate([rows] + [pair_move(rows, step) for step in range(1, pair)], axis=0)

    def pair_scatter(terms):
        total = terms[:rows_local]
        for step in range(1, pair):
            piece = terms[step * rows_local : (step + 1) * rows_local].astype(bf16)
            total = total + pair_move(piece, -step).astype(f32)
        return total

    def tensor_sum(values):
        total = values
        for step in range(1, pair):
            total = total + pair_move(values, step)
        whole = total
        for step in range(1, groups):
            whole = whole + group_move(total, step)
        return whole

    def fetch_direct(weight):
        return [weight] + [group_move(weight, step) for step in range(1, groups)]

    def fetch_spread(weight):
        piece_rows = weight.shape[0] // dp_size
        piece = lax.dynamic_slice_in_dim(weight, dp_at * piece_rows, piece_rows, axis=0)
        return [weight] + [
            lax.all_gather(group_move(piece, step), "dp", axis=0, tiled=True)
            for step in range(1, groups)
        ]

    def send_home(grads):
        total = grads[0]
        for step in range(1, groups):
            total = total + group_move(grads[step].astype(bf16), -step).astype(f32)
        return total.astype(bf16)

    head_cols = qkv_weight.shape[2]
    if head_cols % LANES == 0:
        stages = [[shard] for shard in range(groups)]
    else:
        stages = [list(range(groups))]

    def joined(parts, axis):
        return parts[0] if len(parts) == 1 else jnp.concatenate(parts, axis=axis)

    qkv_of = fetch_direct(qkv_weight)
    qv_bias_of = fetch_direct(qv_bias)
    proj_of = fetch_direct(proj_weight)
    up_of = fetch_spread(up_weight)
    up_bias_of = fetch_direct(up_bias)
    down_of = fetch_spread(down_weight)

    cond_wide = condition.astype(f32)
    cond_sig = jax.nn.sigmoid(cond_wide)
    silu_low = (cond_wide * cond_sig).astype(bf16)
    silu_all = lax.all_gather(silu_low, "dp", axis=0, tiled=True)
    mod_cols = (
        jnp.dot(silu_low, ada_weight, preferred_element_type=f32) + ada_bias.astype(f32)
    ).astype(bf16)
    mod_all = lax.all_gather(mod_cols, "tensor", axis=1, tiled=True)
    mod_row = lax.dynamic_slice_in_dim(mod_all, tensor_at // pair, 1, axis=0).astype(f32)
    shift_attn, scale_attn, gate_attn, shift_mlp, scale_mlp, gate_mlp = [
        mod_row[:, column_set * D : (column_set + 1) * D] for column_set in range(6)
    ]

    tokens_wide = tokens.astype(f32)
    grad_wide = out_grad.astype(f32)
    normed_attn, inv_attn = layer_norm(tokens_wide)
    attn_input = (normed_attn * (1.0 + scale_attn) + shift_attn).astype(bf16)
    attn_pair = pair_gather(attn_input)
    grad_branch_mlp = (gate_mlp * grad_wide).astype(bf16)
    grad_pair = pair_gather(grad_branch_mlp)

    qkv_mats, qkv_rows, heads_out, heads_lse, proj_mats = [], [], [], [], []
    proj_terms = None
    for stage in stages:
        cols = head_cols * len(stage)
        weight = joined([qkv_of[s] for s in stage], 2).reshape(D, 3 * cols)
        bias = joined([qv_bias_of[s] for s in stage], 1)
        shift = jnp.concatenate([bias[0], jnp.zeros_like(bias[0]), bias[1]]).astype(f32)
        rows = (jnp.dot(attn_pair, weight, preferred_element_type=f32) + shift).astype(bf16)
        heads, lse = attend(rows, cols)
        proj = joined([proj_of[s] for s in stage], 0)
        terms = jnp.dot(heads, proj, preferred_element_type=f32)
        proj_terms = terms if proj_terms is None else proj_terms + terms
        qkv_mats.append(weight)
        qkv_rows.append(rows)
        heads_out.append(heads)
        heads_lse.append(lse)
        proj_mats.append(proj)
    branch_attn = pair_scatter(proj_terms) + proj_bias.astype(f32)
    hidden_state = tokens_wide + gate_attn * branch_attn
    normed_mlp, inv_mlp = layer_norm(hidden_state)
    mlp_input = (normed_mlp * (1.0 + scale_mlp) + shift_mlp).astype(bf16)
    mlp_pair = pair_gather(mlp_input)

    pre_acts, hiddens = [], []
    down_terms = None
    for shard in range(groups):
        pre_act = contract(mlp_pair, up_of[shard], 1, 1) + up_bias_of[shard].astype(f32)
        hidden = gelu_tanh(pre_act).astype(bf16)
        terms = jnp.dot(hidden, down_of[shard], preferred_element_type=f32)
        down_terms = terms if down_terms is None else down_terms + terms
        pre_acts.append(pre_act)
        hiddens.append(hidden)
    branch_mlp = pair_scatter(down_terms) + down_bias.astype(f32)
    block_out = (hidden_state + gate_mlp * branch_mlp).astype(bf16)

    down_grads, up_grads, up_bias_sums = [], [], []
    input_terms = None
    for shard in range(groups):
        grad_hidden = contract(grad_pair, down_of[shard], 1, 1)
        grad_pre = jax.vjp(gelu_tanh, pre_acts[shard])[1](grad_hidden)[0].astype(bf16)
        down_grads.append(contract(hiddens[shard], grad_pair, 0, 0))
        up_grads.append(contract(grad_pre, mlp_pair, 0, 0))
        up_bias_sums.append(jnp.sum(grad_pre.astype(f32), axis=0))
        terms = jnp.dot(grad_pre, up_of[shard], preferred_element_type=f32)
        input_terms = terms if input_terms is None else input_terms + terms
    down_sum = lax.psum(send_home(down_grads), "dp")
    up_home, down_sum = lax.optimization_barrier((send_home(up_grads), down_sum))
    up_sum = lax.psum(up_home, "dp")

    grad_mlp_input = pair_scatter(input_terms)
    grad_hidden_state = grad_wide + norm_back(
        grad_mlp_input * (1.0 + scale_mlp), normed_mlp, inv_mlp
    )
    grad_branch_attn = (gate_attn * grad_hidden_state).astype(bf16)
    back_pair = pair_gather(grad_branch_attn)

    proj_grads = [None] * groups
    qkv_grads = [None] * groups
    qv_sums = [None] * groups
    attn_terms = None
    for at in reversed(range(len(stages))):
        stage = stages[at]
        cols = head_cols * len(stage)
        proj_grad = contract(heads_out[at], back_pair, 0, 0)
        grad_heads = contract(back_pair, proj_mats[at], 1, 1).astype(bf16)
        parts = attend_back(qkv_rows[at], grad_heads, heads_lse[at], cols)
        grad_qkv = jnp.concatenate(parts, axis=1)
        qkv_grad = contract(attn_pair, grad_qkv, 0, 0).reshape(D, 3, cols)
        terms = contract(grad_qkv, qkv_mats[at], 1, 1)
        attn_terms = terms if attn_terms is None else attn_terms + terms
        sums = jnp.sum(grad_qkv.astype(f32), axis=0).reshape(3, cols)
        for place, shard in enumerate(stage):
            span = slice(place * head_cols, (place + 1) * head_cols)
            proj_grads[shard] = proj_grad[span]
            qkv_grads[shard] = qkv_grad[:, :, span]
            qv_sums[shard] = jnp.concatenate([sums[0, span], sums[2, span]])
    proj_home, up_sum = lax.optimization_barrier((send_home(proj_grads), up_sum))
    qkv_home = send_home(qkv_grads)

    proj_bias_part = tensor_sum(jnp.sum(grad_branch_attn.astype(f32), axis=0))
    down_bias_part = tensor_sum(jnp.sum(grad_branch_mlp.astype(f32), axis=0))
    small_own = [
        jnp.concatenate([up_bias_sums[shard], qv_sums[shard]]) for shard in range(groups)
    ]
    small_home = small_own[0]
    for step in range(1, groups):
        small_home = small_home + group_move(small_own[step], -step)
    small = jnp.concatenate([small_home, proj_bias_part, down_bias_part]).astype(bf16)

    qkv_sum, proj_sum, small_sum = lax.psum((qkv_home, proj_home, small), "dp")

    grad_attn_input = pair_scatter(attn_terms)
    tokens_grad = grad_hidden_state + norm_back(
        grad_attn_input * (1.0 + scale_attn), normed_attn, inv_attn
    )
    mod_sums = jnp.concatenate(
        [
            jnp.sum(part, axis=0)
            for part in (
                grad_attn_input,
                grad_attn_input * normed_attn,
                grad_hidden_state * branch_attn,
                grad_mlp_input,
                grad_mlp_input * normed_mlp,
                grad_wide * branch_mlp,
            )
        ]
    )
    mod_whole = mod_sums
    for step in range(1, pair):
        mod_whole = mod_whole + pair_move(mod_sums, step)
    share = 6 * D // pair
    mod_share = lax.dynamic_slice_in_dim(
        mod_whole.astype(bf16), (tensor_at % pair) * share, share, axis=0
    )
    mod_grads = lax.all_gather(mod_share[None], ("dp", "tensor"), axis=0, tiled=True)
    mod_grads = mod_grads.reshape(dp_size * latents_local, 6 * D)
    ada_cols = ada_weight.shape[1]
    mod_own = lax.dynamic_slice_in_dim(mod_grads, tensor_at * ada_cols, ada_cols, axis=1)
    ada_weight_grad = contract(silu_all, mod_own, 0, 0)
    ada_bias_grad = jnp.sum(mod_own.astype(f32), axis=0)
    mod_here = lax.dynamic_slice_in_dim(mod_own, dp_at * latents_local, latents_local, axis=0)
    silu_grad = tensor_sum(contract(mod_here, ada_weight, 1, 1))
    condition_grad = silu_grad * (cond_sig * (1.0 + cond_wide * (1.0 - cond_sig)))

    ff_local = up_weight.shape[0]
    small_sum = small_sum.astype(f32)
    at_qv = ff_local
    at_proj = at_qv + 2 * head_cols
    return (
        block_out,
        tokens_grad,
        condition_grad,
        ada_weight_grad,
        ada_bias_grad,
        qkv_sum.astype(f32),
        small_sum[at_qv:at_proj].reshape(2, head_cols),
        proj_sum.astype(f32),
        small_sum[at_proj : at_proj + D],
        up_sum.astype(f32),
        small_sum[:ff_local],
        down_sum.astype(f32),
        small_sum[at_proj + D : at_proj + 2 * D],
    )


def solution(mesh):
    placed = (
        P(("dp", "tensor"), None),
        P("dp", None),
        P(None, "tensor"),
        P("tensor"),
        P(None, None, "tensor"),
        P(None, "tensor"),
        P("tensor", None),
        P(),
        P("tensor", None),
        P("tensor"),
        P("tensor", None),
        P(),
        P(("dp", "tensor"), None),
    )
    return jax.shard_map(
        functools.partial(shards, mesh.shape["dp"], mesh.shape["tensor"]),
        mesh=mesh,
        in_specs=placed,
        out_specs=(
            P(("dp", "tensor"), None),
            P(("dp", "tensor"), None),
            P("dp", None),
            P(None, "tensor"),
            P("tensor"),
            P(None, None, "tensor"),
            P(None, "tensor"),
            P("tensor", None),
            P(),
            P("tensor", None),
            P("tensor"),
            P("tensor", None),
            P(),
        ),
        check_vma=False,
    )
```

time: 900 us -> 586 us (0.65)
  waiting for transfers between devices: 517 us -> 220 us
  Pallas kernels: 0 us -> 51.9 us
  other arithmetic: 82.5 us -> 34.9 us
  blocking collectives: 52.7 us -> 96.8 us
  local copies, waits for them, and re-layouts: 73.8 us -> 30.5 us
  matrix products: 153 us -> 114 us
  starting transfers between devices: 1.2 us -> 18.6 us
    psum x1 -> x3, waiting for transfers between devices: 242 us -> 106 us  [the longest x1 91.7 us: shards(): up_sum = lax.psum(up_home, 'dp')]
    reduce_scatter x4 -> x0, waiting for transfers between devices: 134 us -> none  [the longest x1 47.6 us: shards(): lax.psum_scatter(input_terms.astype(jnp.bfloat16), 'tensor', scatter_dime...]
    all_gather x4 -> x2, waiting for transfers between devices: 117 us -> 16.3 us  [fetch_spread(): lax.all_gather(group_move(piece, step), 'dp', axis=0, tiled=True)]
    ppermute x0 -> x26, waiting for transfers between devices: none -> 97.9 us  [the longest x14 93.4 us: group_move(): return lax.ppermute(values, 'tensor', moves)]
    all_gather x1 -> x3, blocking collectives: 6.28 us -> 79.3 us  [the longest x1 41.7 us: shards(): lax.all_gather(mod_share[None], ('dp', 'tensor'), axis=0, tiled=True)]
    pallas_call x0 -> x4, Pallas kernels: none -> 51.9 us  [the longest x2 30.9 us: attend_back(): pl.pallas_call(attend_back_kernel, grid=(blocks,), in_specs=[column_spec(...]
    dot_general x45 -> x27, matrix products: 153 us -> 114 us  [the longest x18 85.2 us: contract(): lax.dot_general(left, right, (((left_dim,), (right_dim,)), ((), ())), pre...]
    psum x2 -> x1, blocking collectives: 46.4 us -> 17.4 us  [shards(): qkv_sum, proj_sum, small_sum = lax.psum((qkv_home, proj_home, small), 'dp')]
  transfers between devices with their start and end apart: 10 -> 31, of which waited for: 10 -> 12; matrix products, arithmetic and copies ran while one was open for 9% -> 28% of each run, Pallas kernels for 0% -> 9%
where the time goes in v1:
time: 586 us; the launch traced here: 582 us
  waiting for transfers between devices  220 us (38%)
  matrix products  114 us (19%)
  blocking collectives  96.8 us (17%)
  Pallas kernels  51.9 us (9%)
  other arithmetic  34.9 us (6%)
  local copies, waits for them, and re-layouts  30.5 us (5%)
  starting transfers between devices  18.6 us (3%)
  between operations  14.8 us (3%)
    ppermute x14, waiting for transfers between devices, group_move(): return lax.ppermute(values, 'tensor', moves)  93.4 us
    psum x1, waiting for transfers between devices, shards(): up_sum = lax.psum(up_home, 'dp')  91.7 us
    dot_general x18, matrix products, contract(): lax.dot_general(left, right, (((left_dim,), (right_dim,)), ((), ())), pre...  85.2 us
    all_gather x1, blocking collectives, shards(): lax.all_gather(mod_share[None], ('dp', 'tensor'), axis=0, tiled=True)  41.7 us
    all_gather x1, blocking collectives, shards(): silu_all = lax.all_gather(silu_low, 'dp', axis=0, tiled=True)  31.3 us
    pallas_call x2, Pallas kernels, attend_back(): pl.pallas_call(attend_back_kernel, grid=(blocks,), in_specs=[column_spec(...  30.9 us
    pallas_call x2, Pallas kernels, attend(): pl.pallas_call(attend_kernel, grid=(blocks,), in_specs=[column_spec(0), c...  21 us
    psum x1, blocking collectives, shards(): qkv_sum, proj_sum, small_sum = lax.psum((qkv_home, proj_home, small), 'dp')  17.4 us
  transfers between devices with their start and end apart: 31, of which 12 were waited for; matrix products, arithmetic and copies ran while one was open for 28% of the time, Pallas kernels for 9%

profile of v1, /device:TPU:0, one launch (start us, length us, event | category | flops | bytes accessed | tf_op | source)
XLA Modules:
  0.0 582.0 jit_solution(11714622397169131093)
XLA Ops:
  10.3 6.3 %all_gather.15 = bf16[2,6144]{1,0:T(2,128)(2,1)S(1)} all-gather(bf16[2,1536]{1,0:T(2,128)(2,1)S(1)} %fusion.20), channel_id=1, replica_groups=mesh['dp'=8,'tensor'=4] {'tensor'}, dimensions={1}, use_global_device_ids=true | all-gather | bytes 30720 | tf_op jit(solution)/shard_map/all_gather | solution.py:254
  29.2 32.5 %collective-permute-done.2 = bf16[2,256]{1,0:T(2,128)(2,1)S(1)} collective-permute-done((bf16[2,256]{1,0:T(2,128)(2,1)S(1)}, bf16[2,256]{1,0:T(2,128)(2,1)S(1)}, u32[]{:S(2)}, u32[]{:S(2)}) %collective-permute-start.2) | collective-permute-done | bytes 1056 | tf_op jit(solution)/shard_map/ppermute | solution.py:193
  61.8 16.1 %collective-permute-done.6 = bf16[128,1024]{1,0:T(8,128)(2,1)S(1)} collective-permute-done((bf16[128,1024]{1,0:T(8,128)(2,1)S(1)}, bf16[128,1024]{1,0:T(8,128)(2,1)S(1)}, u32[]{:S(2)}, u32[]{:S(2)}) %collective-permute-start.6) | collective-permute-done | bytes 262176 | tf_op jit(solution)/shard_map/ppermute | solution.py:193
  78.8 5.0 add_convert_fusion.4.q_ref.k_ref.v_ref
  83.9 10.3 %attend.2 = (bf16[1024,256]{1,0:T(8,128)(2,1)}, f32[2,2,1024]{2,1,0:T(2,128)}) custom-call(bf16[1024,768]{1,0:T(8,128)(2,1)} %add_convert_fusion.4.q_ref.k_ref.v_ref, bf16[1024,768]{1,0:T(8,128)(2,1)} %add_convert_fusion.4.q_ref.k_ref.v_ref, bf16[1024,768]{1,0:T(8,128)(2,1)} %add_convert_fusion.4.q_ref.k_ref.v_ref), custom_call_target="tpu_custom_call" | custom-call | tf_op jit(solution)/shard_map/attend/pallas_call | solution.py:125
  96.0 5.0 add_convert_fusion.3.q_ref.k_ref.v_ref
  101.0 10.7 %attend.3 = (bf16[1024,256]{1,0:T(8,128)(2,1)}, f32[2,2,1024]{2,1,0:T(2,128)}) custom-call(bf16[1024,768]{1,0:T(8,128)(2,1)} %add_convert_fusion.3.q_ref.k_ref.v_ref, bf16[1024,768]{1,0:T(8,128)(2,1)} %add_convert_fusion.3.q_ref.k_ref.v_ref, bf16[1024,768]{1,0:T(8,128)(2,1)} %add_convert_fusion.3.q_ref.k_ref.v_ref), custom_call_target="tpu_custom_call" | custom-call | tf_op jit(solution)/shard_map/attend/pallas_call | solution.py:125
  124.0 6.9 %collective-permute-done.8 = bf16[128,1024]{1,0:T(8,128)(2,1)S(1)} collective-permute-done((bf16[128,1024]{1,0:T(8,128)(2,1)S(1)}, bf16[128,1024]{1,0:T(8,128)(2,1)S(1)}, u32[]{:S(2)}, u32[]{:S(2)}) %collective-permute-start.8) | collective-permute-done | bytes 262176 | tf_op jit(solution)/shard_map/ppermute | solution.py:193
  137.2 4.6 fusion.58
  141.9 7.9 %convert_reduce_fusion.1 = (f32[1024]{0:T(1024)S(1)}, bf16[1024,1024]{1,0:T(8,128)(2,1)S(1)}) fusion(f32[1024,1024]{1,0:T(8,128)S(1)} %fusion.58, f32[1024]{0:T(1024)S(1)} %convert_element_type.195, bf16[1024,1024]{1,0:T(8,128)(2,1)S(1)} %copy-done.27, bf16[512,1024]{1,0:T(8,128)(2,1)} %collective-permute-done.10, bf16[512,1024]{1,0:T(8,128)(2,1)} %get-tuple-element.59), kind=kOutput, calls=%fused_computation.21 | convolution fusion | flops 2175794176 | bytes 10493952 | tf_op jit(solution)/shard_map/dot_general | solution.py:40
  149.8 4.4 fusion.70
  154.2 4.8 fusion.62
  159.0 7.1 %fusion.57 = f32[1024,1024]{1,0:T(8,128)} fusion(bf16[1024,1024]{1,0:T(8,128)(2,1)} %all-gather.5.cloned.1.call-done, bf16[512,1024]{1,0:T(8,128)(2,1)} %collective-permute-done.5, bf16[512,1024]{1,0:T(8,128)(2,1)} %add_convert_fusion.6), kind=kOutput, calls=%fused_computation.153 | convolution fusion | flops 2151677952 | bytes 8388608 | tf_op jit(solution)/shard_map/dot_general | solution.py:40
  166.0 16.3 %all-gather.7.cloned.1.call-done = bf16[1024,1024]{1,0:T(8,128)(2,1)} async-done(((bf16[128,1024]{1,0:T(8,128)(2,1)}), bf16[1024,1024]{1,0:T(8,128)(2,1)}) %all-gather.7.cloned.1.call-update) | async-done | bytes 2097168 | tf_op jit(solution)/shard_map/all_gather | solution.py:221
  182.3 8.4 %convert_reduce_fusion = (f32[1024]{0:T(1024)S(1)}, bf16[1024,1024]{1,0:T(8,128)(2,1)S(1)}) fusion(f32[1024,1024]{1,0:T(8,128)} %fusion.57, f32[1024]{0:T(1024)S(1)} %convert_element_type.197, bf16[1024,1024]{1,0:T(8,128)(2,1)} %all-gather.7.cloned.1.call-done, bf16[512,1024]{1,0:T(8,128)(2,1)} %collective-permute-done.10, ...), kind=kOutput, calls=%fused_computation.20 | convolution fusion | flops 2175794176 | bytes 10493952 | tf_op jit(solution)/shard_map/dot_general | solution.py:40
  198.1 4.9 convolution_convert_fusion
  210.6 5.5 convolution_convert_fusion.1
  217.4 34.3 %collective-permute-done.20 = f32[1024]{0:T(1024)S(1)} collective-permute-done((f32[1024]{0:T(1024)S(1)}, f32[1024]{0:T(1024)S(1)}, u32[]{:S(2)}, u32[]{:S(2)}) %collective-permute-start.20) | collective-permute-done | bytes 4128 | tf_op jit(solution)/shard_map/ppermute | solution.py:193
  251.7 6.0 %add_convert_fusion = bf16[1024,1024]{1,0:T(8,128)(2,1)} fusion(bf16[1024,1024]{1,0:T(8,128)(2,1)S(1)} %collective-permute-done.25, bf16[512,1024]{1,0:T(8,128)(2,1)} %collective-permute-done.10, bf16[512,1024]{1,0:T(8,128)(2,1)} %get-tuple-element.59, f32[1024,1024]{1,0:T(8,128)S(1)} %copy-done.37, f32[1024]{0:T(1024)S(1)} %convert_element_type.195), kind=kOutput, calls=%fused_computation.18 | convolution fusion | flops 2165309440 | bytes 10489856 | tf_op jit(solution)/shard_map/dot_general | solution.py:40
  266.1 15.4 %attend_back.2 = (bf16[1024,256]{1,0:T(8,128)(2,1)}, bf16[1024,256]{1,0:T(8,128)(2,1)}, bf16[1024,256]{1,0:T(8,128)(2,1)}) custom-call(bf16[1024,768]{1,0:T(8,128)(2,1)} %add_convert_fusion.3.q_ref.k_ref.v_ref, bf16[1024,768]{1,0:T(8,128)(2,1)} %add_convert_fusion.3.q_ref.k_ref.v_ref, bf16[1024,768]{1,0:T(8,128)(2,1)} %add_convert_fusion.3.q_ref.k_ref.v_ref, ...), custom_call_target="tpu_custom_call" | custom-call | tf_op jit(solution)/shard_map/attend_back/pallas_call | solution.py:143
  287.9 15.6 %attend_back.3 = (bf16[1024,256]{1,0:T(8,128)(2,1)}, bf16[1024,256]{1,0:T(8,128)(2,1)}, bf16[1024,256]{1,0:T(8,128)(2,1)}) custom-call(bf16[1024,768]{1,0:T(8,128)(2,1)} %add_convert_fusion.4.q_ref.k_ref.v_ref, bf16[1024,768]{1,0:T(8,128)(2,1)} %add_convert_fusion.4.q_ref.k_ref.v_ref, bf16[1024,768]{1,0:T(8,128)(2,1)} %add_convert_fusion.4.q_ref.k_ref.v_ref, ...), custom_call_target="tpu_custom_call" | custom-call | tf_op jit(solution)/shard_map/attend_back/pallas_call | solution.py:143
  305.4 4.5 convolution_convert_fusion.2
  317.8 5.6 fusion.59
  323.4 3.7 copy.39
  327.1 3.8 fusion.71
  338.7 6.0 %add_convert_fusion.1 = bf16[1024,1024]{1,0:T(8,128)(2,1)} fusion(bf16[1024,1024]{1,0:T(8,128)(2,1)} %collective-permute-done.24, bf16[1024,1024]{1,0:T(8,128)(2,1)S(1)} %copy-done.40, bf16[512,1024]{1,0:T(8,128)(2,1)} %collective-permute-done.5, bf16[512,1024]{1,0:T(8,128)(2,1)} %add_convert_fusion.6), kind=kOutput, calls=%fused_computation.19 | convolution fusion | flops 2154823680 | bytes 8388608 | tf_op jit(solution)/shard_map/dot_general | solution.py:40
  344.6 14.1 %all-reduce.5.cloned.1.call-done = bf16[1024,1024]{1,0:T(8,128)(2,1)} async-done(((bf16[1024,1024]{1,0:T(8,128)(2,1)}), bf16[1024,1024]{1,0:T(8,128)(2,1)}) %all-reduce.5.cloned.1.call-update) | async-done | bytes 2097168 | tf_op jit(solution)/shard_map/psum | solution.py:313
  365.6 3.9 multiply_reduce_fusion.1
  372.7 91.7 %all-reduce.7.cloned.1.call-done = bf16[1024,1024]{1,0:T(8,128)(2,1)} async-done(((bf16[1024,1024]{1,0:T(8,128)(2,1)}), bf16[1024,1024]{1,0:T(8,128)(2,1)}) %all-reduce.7.cloned.1.call-update) | async-done | bytes 2097168 | tf_op jit(solution)/shard_map/psum | solution.py:315
  465.8 41.7 %all-gather = bf16[98304]{0:T(1024)(128)(2,1)S(1)} all-gather(bf16[3072]{0:T(1024)(128)(2,1)S(1)} %fusion.36), channel_id=2, replica_groups=mesh['dp'=8,'tensor'=4] {'dp','tensor'}, dimensions={0}, use_global_device_ids=true | all-gather | bytes 202752 | tf_op jit(solution)/shard_map/all_gather | solution.py:383
  508.9 17.4 %psum.36 = bf16[3584]{0:T(1024)(128)(2,1)S(1)} all-reduce(bf16[3584]{0:T(1024)(128)(2,1)S(1)} %pad_maximum_fusion.5), channel_id=1, replica_groups=mesh['dp'=8,'tensor'=4] {'dp'}, use_global_device_ids=true, to_apply=%region_22.23 | all-reduce | flops 3584 | bytes 14336 | tf_op jit(solution)/shard_map/psum | solution.py:357
  530.7 31.3 %all-gather.1 = bf16[8,2,1024]{2,1,0:T(2,128)(2,1)S(1)} all-gather(bf16[1,2,1024]{2,1,0:T(2,128)(2,1)S(1)} %get-tuple-element.82), channel_id=1, replica_groups=mesh['dp'=8,'tensor'=4] {'dp'}, dimensions={0}, use_global_device_ids=true | all-gather | bytes 36864 | tf_op jit(solution)/shard_map/all_gather | solution.py:250
  (229 shorter events, 115.6 us)
Async XLA Ops:
  7.2 151.8 %all-gather.5.cloned.1.call-start = ((), (), s32[]{:S(2)}) async-start(), calls=%async_computation | async-start | bytes 2359296 | tf_op jit(solution)/shard_map/all_gather | solution.py:221
  21.2 57.6 %collective-permute-start = (bf16[512,1024]{1,0:T(8,128)(2,1)}, bf16[512,1024]{1,0:T(8,128)(2,1)}, u32[]{:S(2)}, u32[]{:S(2)}) collective-permute-start(bf16[512,1024]{1,0:T(8,128)(2,1)} %fusion.22), channel_id=1, source_target_pairs={{0,1},{1,0},{2,3},{3,2},{4,5},{5,4},{6,7},{7,6},{8,9},{9,8},{10,11... | collective-permute-start | bytes 3145736 | tf_op jit(solution)/shard_map/ppermute | solution.py:189
  24.1 71.8 %collective-permute-start.1 = (bf16[1024,3,256]{0,2,1:T(8,128)(2,1)}, bf16[1024,3,256]{0,2,1:T(8,128)(2,1)}, u32[]{:S(2)}, u32[]{:S(2)}) collective-permute-start(bf16[1024,3,256]{0,2,1:T(8,128)(2,1)} %copy.36), channel_id=1, source_target_pairs={{0,2},{1,3},{2,0},{3,1},{4,6},{5,7},{6,4},{7,5},{8,10},{9,11},{10,... | collective-permute-start | bytes 4718600 | tf_op jit(solution)/shard_map/ppermute | solution.py:193
  26.1 35.7 %collective-permute-start.2 = (bf16[2,256]{1,0:T(2,128)(2,1)S(1)}, bf16[2,256]{1,0:T(2,128)(2,1)S(1)}, u32[]{:S(2)}, u32[]{:S(2)}) collective-permute-start(bf16[2,256]{1,0:T(2,128)(2,1)S(1)} %copy-done.29), channel_id=1, source_target_pairs={{0,2},{1,3},{2,0},{3,1},{4,6},{5,7},{6,4},{7,5},{8,10},{9,11},{10,... | collective-permute-start | bytes 3080 | tf_op jit(solution)/shard_map/ppermute | solution.py:193
  26.2 85.5 %collective-permute-start.3 = (bf16[256,1024]{1,0:T(8,128)(2,1)}, bf16[256,1024]{1,0:T(8,128)(2,1)}, u32[]{:S(2)}, u32[]{:S(2)}) collective-permute-start(bf16[256,1024]{1,0:T(8,128)(2,1)} %param.19), channel_id=1, source_target_pairs={{0,2},{1,3},{2,0},{3,1},{4,6},{5,7},{6,4},{7,5},{8,10},{9,11},{10,... | collective-permute-start | bytes 1572872 | tf_op jit(solution)/shard_map/ppermute | solution.py:193
  29.1 48.8 %collective-permute-start.6 = (bf16[128,1024]{1,0:T(8,128)(2,1)S(1)}, bf16[128,1024]{1,0:T(8,128)(2,1)S(1)}, u32[]{:S(2)}, u32[]{:S(2)}) collective-permute-start(bf16[128,1024]{1,0:T(8,128)(2,1)S(1)} %constant_dynamic-slice_fusion.1), channel_id=1, source_target_pairs={{0,2},{1,3},{2,0},{3,1},{4,6},{5,7},{6,4},{7,5},{8,10},{9,11},{10,... | collective-permute-start | bytes 786440 | tf_op jit(solution)/shard_map/ppermute | solution.py:193
  78.6 103.7 %all-gather.7.cloned.1.call-start = ((), (), s32[]{:S(2)}) async-start(), calls=%async_computation.1 | async-start | bytes 2359296 | tf_op jit(solution)/shard_map/all_gather | solution.py:221
  113.8 2.7 collective-permute-start.4
  119.2 18.0 %collective-permute-start.5 = (bf16[512,1024]{1,0:T(8,128)(2,1)}, bf16[512,1024]{1,0:T(8,128)(2,1)}, u32[]{:S(2)}, u32[]{:S(2)}) collective-permute-start(bf16[512,1024]{1,0:T(8,128)(2,1)} %add_convert_fusion.6), channel_id=1, source_target_pairs={{0,1},{1,0},{2,3},{3,2},{4,5},{5,4},{6,7},{7,6},{8,9},{9,8},{10,11... | collective-permute-start | bytes 3145736 | tf_op jit(solution)/shard_map/ppermute | solution.py:189
  121.1 20.7 %collective-permute-start.10 = (bf16[512,1024]{1,0:T(8,128)(2,1)}, bf16[512,1024]{1,0:T(8,128)(2,1)}, u32[]{:S(2)}, u32[]{:S(2)}) collective-permute-start(bf16[512,1024]{1,0:T(8,128)(2,1)} %get-tuple-element.59), channel_id=1, source_target_pairs={{0,1},{1,0},{2,3},{3,2},{4,5},{5,4},{6,7},{7,6},{8,9},{9,8},{10,11... | collective-permute-start | bytes 3145736 | tf_op jit(solution)/shard_map/ppermute | solution.py:189
  122.2 8.6 %collective-permute-start.8 = (bf16[128,1024]{1,0:T(8,128)(2,1)S(1)}, bf16[128,1024]{1,0:T(8,128)(2,1)S(1)}, u32[]{:S(2)}, u32[]{:S(2)}) collective-permute-start(bf16[128,1024]{1,0:T(8,128)(2,1)S(1)} %constant_dynamic-slice_fusion), channel_id=1, source_target_pairs={{0,2},{1,3},{2,0},{3,1},{4,6},{5,7},{6,4},{7,5},{8,10},{9,11},{10,... | collective-permute-start | bytes 786440 | tf_op jit(solution)/shard_map/ppermute | solution.py:193
  131.6 227.1 %all-reduce.5.cloned.1.call-start = ((), (), s32[]{:S(2)}) async-start(), calls=%async_computation.2 | async-start | bytes 4194304 | tf_op jit(solution)/shard_map/psum | solution.py:313
  131.6 3.7 collective-permute-start.21
  131.7 3.7 collective-permute-start.7
  135.4 73.6 %collective-permute-start.22 = (f32[1024]{0:T(1024)S(1)}, f32[1024]{0:T(1024)S(1)}, u32[]{:S(2)}, u32[]{:S(2)}) collective-permute-start(f32[1024]{0:T(1024)S(1)} %add.284), channel_id=1, source_target_pairs={{0,2},{1,3},{2,0},{3,1},{4,6},{5,7},{6,4},{7,5},{8,10},{9,11},{10,... | collective-permute-start | bytes 12296 | tf_op jit(solution)/shard_map/ppermute | solution.py:193
  193.2 11.4 %collective-permute-start.11 = (bf16[512,1024]{1,0:T(8,128)(2,1)S(1)}, bf16[512,1024]{1,0:T(8,128)(2,1)S(1)}, u32[]{:S(2)}, u32[]{:S(2)}) collective-permute-start(bf16[512,1024]{1,0:T(8,128)(2,1)S(1)} %slice.190), channel_id=1, source_target_pairs={{0,1},{1,0},{2,3},{3,2},{4,5},{5,4},{6,7},{7,6},{8,9},{9,8},{10,11... | collective-permute-start | bytes 3145736 | tf_op jit(solution)/shard_map/ppermute | solution.py:189
  198.0 7.6 %collective-permute-start.9 = (bf16[512,1024]{1,0:T(8,128)(2,1)S(1)}, bf16[512,1024]{1,0:T(8,128)(2,1)S(1)}, u32[]{:S(2)}, u32[]{:S(2)}) collective-permute-start(bf16[512,1024]{1,0:T(8,128)(2,1)S(1)} %slice.191), channel_id=1, source_target_pairs={{0,1},{1,0},{2,3},{3,2},{4,5},{5,4},{6,7},{7,6},{8,9},{9,8},{10,11... | collective-permute-start | bytes 3145736 | tf_op jit(solution)/shard_map/ppermute | solution.py:189
  203.0 48.7 %collective-permute-start.25 = (bf16[1024,1024]{1,0:T(8,128)(2,1)S(1)}, bf16[1024,1024]{1,0:T(8,128)(2,1)S(1)}, u32[]{:S(2)}, u32[]{:S(2)}) collective-permute-start(bf16[1024,1024]{1,0:T(8,128)(2,1)S(1)} %convolution_convert_fusion), channel_id=1, source_target_pairs={{0,2},{1,3},{2,0},{3,1},{4,6},{5,7},{6,4},{7,5},{8,10},{9,11},{10,... | collective-permute-start | bytes 6291464 | tf_op jit(solution)/shard_map/ppermute | solution.py:193
  208.9 1.2 collective-permute-start.19
  210.1 41.6 %collective-permute-start.20 = (f32[1024]{0:T(1024)S(1)}, f32[1024]{0:T(1024)S(1)}, u32[]{:S(2)}, u32[]{:S(2)}) collective-permute-start(f32[1024]{0:T(1024)S(1)} %add.282), channel_id=1, source_target_pairs={{0,2},{1,3},{2,0},{3,1},{4,6},{5,7},{6,4},{7,5},{8,10},{9,11},{10,... | collective-permute-start | bytes 12296 | tf_op jit(solution)/shard_map/ppermute | solution.py:193
  216.2 122.1 %collective-permute-start.24 = (bf16[1024,1024]{1,0:T(8,128)(2,1)}, bf16[1024,1024]{1,0:T(8,128)(2,1)}, u32[]{:S(2)}, u32[]{:S(2)}) collective-permute-start(bf16[1024,1024]{1,0:T(8,128)(2,1)} %convolution_convert_fusion.1), channel_id=1, source_target_pairs={{0,2},{1,3},{2,0},{3,1},{4,6},{5,7},{6,4},{7,5},{8,10},{9,11},{10,... | collective-permute-start | bytes 6291464 | tf_op jit(solution)/shard_map/ppermute | solution.py:193
  217.4 40.8 %collective-permute-start.12 = (bf16[512,1024]{1,0:T(8,128)(2,1)}, bf16[512,1024]{1,0:T(8,128)(2,1)}, u32[]{:S(2)}, u32[]{:S(2)}) collective-permute-start(bf16[512,1024]{1,0:T(8,128)(2,1)} %get-tuple-element.65), channel_id=1, source_target_pairs={{0,1},{1,0},{2,3},{3,2},{4,5},{5,4},{6,7},{7,6},{8,9},{9,8},{10,11... | collective-permute-start | bytes 3145736 | tf_op jit(solution)/shard_map/ppermute | solution.py:189
  257.7 206.7 %all-reduce.7.cloned.1.call-start = ((), (), s32[]{:S(2)}) async-start(), calls=%async_computation.3 | async-start | bytes 4194304 | tf_op jit(solution)/shard_map/psum | solution.py:315
  261.4 97.4 %collective-permute-start.23 = (bf16[256,1024]{1,0:T(8,128)(2,1)}, bf16[256,1024]{1,0:T(8,128)(2,1)}, u32[]{:S(2)}, u32[]{:S(2)}) collective-permute-start(bf16[256,1024]{1,0:T(8,128)(2,1)} %convolution_convert_fusion.3), channel_id=1, source_target_pairs={{0,2},{1,3},{2,0},{3,1},{4,6},{5,7},{6,4},{7,5},{8,10},{9,11},{10,... | collective-permute-start | bytes 1572872 | tf_op jit(solution)/shard_map/ppermute | solution.py:193
  284.1 180.4 %collective-permute-start.18 = (f32[1536]{0:T(1024)S(1)}, f32[1536]{0:T(1024)S(1)}, u32[]{:S(2)}, u32[]{:S(2)}) collective-permute-start(f32[1536]{0:T(1024)S(1)} %pad_maximum_fusion.4), channel_id=1, source_target_pairs={{0,2},{1,3},{2,0},{3,1},{4,6},{5,7},{6,4},{7,5},{8,10},{9,11},{10,... | collective-permute-start | bytes 18440 | tf_op jit(solution)/shard_map/ppermute | solution.py:193
  312.5 57.0 %collective-permute-start.17 = (bf16[1024,3,256]{2,0,1:T(8,128)(2,1)}, bf16[1024,3,256]{2,0,1:T(8,128)(2,1)}, u32[]{:S(2)}, u32[]{:S(2)}) collective-permute-start(bf16[1024,3,256]{2,0,1:T(8,128)(2,1)} %copy.38), channel_id=1, source_target_pairs={{0,2},{1,3},{2,0},{3,1},{4,6},{5,7},{6,4},{7,5},{8,10},{9,11},{10,... | collective-permute-start | bytes 4718600 | tf_op jit(solution)/shard_map/ppermute | solution.py:193
  337.4 25.0 %collective-permute-start.13 = (bf16[512,1024]{1,0:T(8,128)(2,1)}, bf16[512,1024]{1,0:T(8,128)(2,1)}, u32[]{:S(2)}, u32[]{:S(2)}) collective-permute-start(bf16[512,1024]{1,0:T(8,128)(2,1)} %slice.189), channel_id=1, source_target_pairs={{0,1},{1,0},{2,3},{3,2},{4,5},{5,4},{6,7},{7,6},{8,9},{9,8},{10,11... | collective-permute-start | bytes 3145736 | tf_op jit(solution)/shard_map/ppermute | solution.py:189
  358.8 212.0 %all-reduce.9.cloned.1.call-start = ((), (), s32[]{:S(2)}) async-start(), calls=%async_computation.4 | async-start | bytes 4194304 | tf_op jit(solution)/shard_map/psum | solution.py:357
  464.4 65.6 %copy-start.28 = (bf16[2,1024]{1,0:T(2,128)(2,1)S(1)}, bf16[2,1024]{1,0:T(2,128)(2,1)}, u32[]{:S(2)}) copy-start(bf16[2,1024]{1,0:T(2,128)(2,1)} %param.14) | copy-start | bytes 12292
  464.5 1.3 collective-permute-start.14
  508.5 17.8 %collective-permute-start.15 = (f32[2,1024]{1,0:T(2,128)S(1)}, f32[2,1024]{1,0:T(2,128)S(1)}, u32[]{:S(2)}, u32[]{:S(2)}) collective-permute-start(f32[2,1024]{1,0:T(2,128)S(1)} %fusion.45), channel_id=1, source_target_pairs={{0,1},{1,0},{2,3},{3,2},{4,5},{5,4},{6,7},{7,6},{8,9},{9,8},{10,11... | collective-permute-start | bytes 24584 | tf_op jit(solution)/shard_map/ppermute | solution.py:189
  526.3 3.7 collective-permute-start.16
  (41 other events, 237.1 us)
Sparse Core Ops, SparseCore 0:
  78.7 50.5 all-gather.4
  132.0 50.2 all-gather.6
  257.8 100.8 all-reduce.4
  362.8 101.5 all-reduce.6
  467.9 102.5 all-reduce.8

commit v2 on v1

--- a/solution.py
+++ b/solution.py
@@ -47,17 +47,17 @@
     return (lane >= head * HD) & (lane < (head + 1) * HD)
 
 
-def attend_kernel(q_ref, k_ref, v_ref, out_ref, lse_ref):
+def attend_kernel(qkv_ref, out_ref, lse_ref):
     heads = LANES // HD
-    keys = k_ref[...]
-    values = v_ref[...]
+    keys = qkv_ref[:, LANES : 2 * LANES]
+    values = qkv_ref[:, 2 * LANES :]
     masks = [head_mask(keys.shape, head) for head in range(heads)]
     zero = jnp.zeros_like(keys)
     keys_of = [jnp.where(mask, keys, zero) for mask in masks]
     values_of = [jnp.where(mask, values, zero) for mask in masks]
     for start in range(0, SEQ, query_block):
         rows = pl.ds(start, query_block)
-        query = q_ref[rows, :] * jnp.bfloat16(score_scale)
+        query = qkv_ref[rows, :LANES] * jnp.bfloat16(score_scale)
         total = None
         for head in range(heads):
             scores = contract(keys_of[head], query, 1, 1)
@@ -71,19 +71,17 @@
         out_ref[rows, :] = total.astype(jnp.bfloat16)
 
 
-def attend_back_kernel(
-    q_ref, k_ref, v_ref, do_ref, lse_ref, dq_ref, dk_ref, dv_ref, dk_acc, dv_acc
-):
+def attend_back_kernel(qkv_ref, do_ref, lse_ref, dqkv_ref, dk_acc, dv_acc):
     heads = LANES // HD
-    keys = k_ref[...]
-    values = v_ref[...]
+    keys = qkv_ref[:, LANES : 2 * LANES]
+    values = qkv_ref[:, 2 * LANES :]
     mask_keys = [head_mask(keys.shape, head) for head in range(heads)]
     zero = jnp.zeros_like(keys)
     keys_of = [jnp.where(mask, keys, zero) for mask in mask_keys]
     values_of = [jnp.where(mask, values, zero) for mask in mask_keys]
     for start in range(0, SEQ, query_block):
         rows = pl.ds(start, query_block)
-        query = q_ref[rows, :] * jnp.bfloat16(score_scale)
+        query = qkv_ref[rows, :LANES] * jnp.bfloat16(score_scale)
         grad = do_ref[rows, :]
         mask_query = [head_mask(query.shape, head) for head in range(heads)]
         none = jnp.zeros_like(query)
@@ -104,58 +102,52 @@
             dv_new = dv_part if dv_new is None else dv_new + dv_part
             dk_new = dk_part if dk_new is None else dk_new + dk_part
             total = dq_part if total is None else total + dq_part
-        dq_ref[rows, :] = (total * score_scale).astype(jnp.bfloat16)
+        dqkv_ref[rows, :LANES] = (total * score_scale).astype(jnp.bfloat16)
         if start == 0:
             dk_acc[...] = dk_new
             dv_acc[...] = dv_new
         else:
             dk_acc[...] += dk_new
             dv_acc[...] += dv_new
-    dk_ref[...] = dk_acc[...].astype(jnp.bfloat16)
-    dv_ref[...] = dv_acc[...].astype(jnp.bfloat16)
-
-
-def column_spec(offset):
-    return pl.BlockSpec((SEQ, LANES), lambda step: (0, step + offset))
-
-
-def attend(qkv_rows, head_cols):
-    blocks = head_cols // LANES
-    lse_spec = pl.BlockSpec((1, LANES // HD, SEQ), lambda step: (step, 0, 0))
+    dqkv_ref[:, LANES : 2 * LANES] = dk_acc[...].astype(jnp.bfloat16)
+    dqkv_ref[:, 2 * LANES :] = dv_acc[...].astype(jnp.bfloat16)
+
+
+def column_spec(width):
+    return pl.BlockSpec((SEQ, width), lambda step: (0, step))
+
+
+lse_spec = pl.BlockSpec((1, LANES // HD, SEQ), lambda step: (step, 0, 0))
+
+
+def attend(qkv_rows):
+    blocks = qkv_rows.shape[1] // (3 * LANES)
     return pl.pallas_call(
         attend_kernel,
         grid=(blocks,),
-        in_specs=[column_spec(0), column_spec(blocks), column_spec(2 * blocks)],
-        out_specs=[column_spec(0), lse_spec],
+        in_specs=[column_spec(3 * LANES)],
+        out_specs=[column_spec(LANES), lse_spec],
         out_shape=[
-            jax.ShapeDtypeStruct((SEQ, head_cols), jnp.bfloat16),
+            jax.ShapeDtypeStruct((SEQ, blocks * LANES), jnp.bfloat16),
             jax.ShapeDtypeStruct((blocks, LANES // HD, SEQ), jnp.float32),
         ],
         compiler_params=pltpu.CompilerParams(vmem_limit_bytes=vmem_limit),
         name="attend",
-    )(qkv_rows, qkv_rows, qkv_rows)
-
-
-def attend_back(qkv_rows, grad_heads, lse, head_cols):
-    blocks = head_cols // LANES
-    lse_spec = pl.BlockSpec((1, LANES // HD, SEQ), lambda step: (step, 0, 0))
-    part = jax.ShapeDtypeStruct((SEQ, head_cols), jnp.bfloat16)
+    )(qkv_rows)
+
+
+def attend_back(qkv_rows, grad_heads, lse):
+    blocks = qkv_rows.shape[1] // (3 * LANES)
     return pl.pallas_call(
         attend_back_kernel,
         grid=(blocks,),
-        in_specs=[
-            column_spec(0),
-            column_spec(blocks),
-            column_spec(2 * blocks),
-            column_spec(0),
-            lse_spec,
-        ],
-        out_specs=[column_spec(0)] * 3,
-        out_shape=[part] * 3,
+        in_specs=[column_spec(3 * LANES), column_spec(LANES), lse_spec],
+        out_specs=column_spec(3 * LANES),
+        out_shape=jax.ShapeDtypeStruct(qkv_rows.shape, jnp.bfloat16),
         scratch_shapes=[pltpu.VMEM((SEQ, LANES), jnp.float32)] * 2,
         compiler_params=pltpu.CompilerParams(vmem_limit_bytes=vmem_limit),
         name="attend_back",
-    )(qkv_rows, qkv_rows, qkv_rows, grad_heads, lse)
+    )(qkv_rows, grad_heads, lse)
 
 
 def shards(
@@ -214,19 +206,36 @@
     def fetch_direct(weight):
         return [weight] + [group_move(weight, step) for step in range(1, groups)]
 
-    def fetch_spread(weight):
+    def spread_pieces(weight):
         piece_rows = weight.shape[0] // dp_size
         piece = lax.dynamic_slice_in_dim(weight, dp_at * piece_rows, piece_rows, axis=0)
-        return [weight] + [
-            lax.all_gather(group_move(piece, step), "dp", axis=0, tiled=True)
-            for step in range(1, groups)
-        ]
-
-    def send_home(grads):
-        total = grads[0]
-        for step in range(1, groups):
-            total = total + group_move(grads[step].astype(bf16), -step).astype(f32)
+        return [group_move(piece, step) for step in range(1, groups)]
+
+    def spread_gather(pieces):
+        return [lax.all_gather(piece, "dp", axis=0, tiled=True) for piece in pieces]
+
+    def away(grads):
+        return [group_move(grads[step].astype(bf16), -step) for step in range(1, groups)]
+
+    def home(own, arrived):
+        total = own
+        for piece in arrived:
+            total = total + piece.astype(f32)
         return total.astype(bf16)
+
+    def dp_sum(values):
+        part = lax.psum_scatter(values, "dp", scatter_dimension=0, tiled=True)
+        return lax.all_gather(part, "dp", axis=0, tiled=True)
+
+    def dp_gather(rows):
+        step = 1
+        while step < dp_size:
+            moves = [(i, i ^ step) for i in range(dp_size)]
+            rows = jnp.concatenate([rows, lax.ppermute(rows, "dp", moves)], axis=0)
+            step *= 2
+        return rows
+
+    hold = lax.optimization_barrier
 
     head_cols = qkv_weight.shape[2]
     if head_cols % LANES == 0:
@@ -237,17 +246,23 @@
     def joined(parts, axis):
         return parts[0] if len(parts) == 1 else jnp.concatenate(parts, axis=axis)
 
-    qkv_of = fetch_direct(qkv_weight)
-    qv_bias_of = fetch_direct(qv_bias)
+    ff_local = up_weight.shape[0]
+    if head_cols % LANES == 0:
+        blocks = head_cols // LANES
+        qkv_flat = qkv_weight.reshape(D, 3, blocks, LANES).swapaxes(1, 2).reshape(D, 3 * head_cols)
+        qkv_of = fetch_direct(qkv_flat)
+    else:
+        qkv_of = fetch_direct(qkv_weight)
     proj_of = fetch_direct(proj_weight)
-    up_of = fetch_spread(up_weight)
-    up_bias_of = fetch_direct(up_bias)
-    down_of = fetch_spread(down_weight)
+    small_of = fetch_direct(jnp.concatenate([up_bias, qv_bias.reshape(-1)]))
+    qv_bias_of = [part[ff_local:].reshape(2, head_cols) for part in small_of]
+    up_bias_of = [part[:ff_local] for part in small_of]
+    up_pieces = spread_pieces(up_weight)
+    down_pieces = spread_pieces(down_weight)
 
     cond_wide = condition.astype(f32)
     cond_sig = jax.nn.sigmoid(cond_wide)
     silu_low = (cond_wide * cond_sig).astype(bf16)
-    silu_all = lax.all_gather(silu_low, "dp", axis=0, tiled=True)
     mod_cols = (
         jnp.dot(silu_low, ada_weight, preferred_element_type=f32) + ada_bias.astype(f32)
     ).astype(bf16)
@@ -261,19 +276,33 @@
     grad_wide = out_grad.astype(f32)
     normed_attn, inv_attn = layer_norm(tokens_wide)
     attn_input = (normed_attn * (1.0 + scale_attn) + shift_attn).astype(bf16)
+    attn_input, up_pieces, down_pieces = hold((attn_input, up_pieces, down_pieces))
+    up_far = spread_gather(up_pieces)
+    down_far = spread_gather(down_pieces)
     attn_pair = pair_gather(attn_input)
     grad_branch_mlp = (gate_mlp * grad_wide).astype(bf16)
-    grad_pair = pair_gather(grad_branch_mlp)
 
     qkv_mats, qkv_rows, heads_out, heads_lse, proj_mats = [], [], [], [], []
     proj_terms = None
-    for stage in stages:
+    for at, stage in enumerate(stages):
         cols = head_cols * len(stage)
-        weight = joined([qkv_of[s] for s in stage], 2).reshape(D, 3 * cols)
         bias = joined([qv_bias_of[s] for s in stage], 1)
-        shift = jnp.concatenate([bias[0], jnp.zeros_like(bias[0]), bias[1]]).astype(f32)
+        shift = jnp.stack([bias[0], jnp.zeros_like(bias[0]), bias[1]]).astype(f32)
+        shift = shift.reshape(3, cols // LANES, LANES).swapaxes(0, 1).reshape(3 * cols)
+        if head_cols % LANES == 0:
+            weight = qkv_of[stage[0]]
+        else:
+            weight = joined([qkv_of[s] for s in stage], 2)
+            weight = weight.reshape(D, 3, cols // LANES, LANES).swapaxes(1, 2)
+            weight = weight.reshape(D, 3 * cols)
         rows = (jnp.dot(attn_pair, weight, preferred_element_type=f32) + shift).astype(bf16)
-        heads, lse = attend(rows, cols)
+        heads, lse = attend(rows)
+        if at == 0 and len(stages) > 1:
+            heads, qkv_of[1:], proj_of[1:], small_of = hold(
+                (heads, qkv_of[1:], proj_of[1:], small_of)
+            )
+        if at == len(stages) - 1:
+            heads, up_far, down_far = hold((heads, up_far, down_far))
         proj = joined([proj_of[s] for s in stage], 0)
         terms = jnp.dot(heads, proj, preferred_element_type=f32)
         proj_terms = terms if proj_terms is None else proj_terms + terms
@@ -282,6 +311,9 @@
         heads_out.append(heads)
         heads_lse.append(lse)
         proj_mats.append(proj)
+    up_of = [up_weight] + list(up_far)
+    down_of = [down_weight] + list(down_far)
+    grad_pair = pair_gather(grad_branch_mlp)
     branch_attn = pair_scatter(proj_terms) + proj_bias.astype(f32)
     hidden_state = tokens_wide + gate_attn * branch_attn
     normed_mlp, inv_mlp = layer_norm(hidden_state)
@@ -300,19 +332,19 @@
     branch_mlp = pair_scatter(down_terms) + down_bias.astype(f32)
     block_out = (hidden_state + gate_mlp * branch_mlp).astype(bf16)
 
-    down_grads, up_grads, up_bias_sums = [], [], []
+    down_grads, up_grads, up_bias_sums = [None] * groups, [None] * groups, [None] * groups
     input_terms = None
-    for shard in range(groups):
+    for shard in reversed(range(groups)):
+        down_grads[shard] = contract(hiddens[shard], grad_pair, 0, 0)
+    down_away = away(down_grads)
+    for shard in reversed(range(groups)):
         grad_hidden = contract(grad_pair, down_of[shard], 1, 1)
         grad_pre = jax.vjp(gelu_tanh, pre_acts[shard])[1](grad_hidden)[0].astype(bf16)
-        down_grads.append(contract(hiddens[shard], grad_pair, 0, 0))
-        up_grads.append(contract(grad_pre, mlp_pair, 0, 0))
-        up_bias_sums.append(jnp.sum(grad_pre.astype(f32), axis=0))
+        up_grads[shard] = contract(grad_pre, mlp_pair, 0, 0)
+        up_bias_sums[shard] = jnp.sum(grad_pre.astype(f32), axis=0)
         terms = jnp.dot(grad_pre, up_of[shard], preferred_element_type=f32)
         input_terms = terms if input_terms is None else input_terms + terms
-    down_sum = lax.psum(send_home(down_grads), "dp")
-    up_home, down_sum = lax.optimization_barrier((send_home(up_grads), down_sum))
-    up_sum = lax.psum(up_home, "dp")
+    up_away = away(up_grads)
 
     grad_mlp_input = pair_scatter(input_terms)
     grad_hidden_state = grad_wide + norm_back(
@@ -320,6 +352,8 @@
     )
     grad_branch_attn = (gate_attn * grad_hidden_state).astype(bf16)
     back_pair = pair_gather(grad_branch_attn)
+    back_pair, down_own, down_away = hold((back_pair, down_grads[0], down_away))
+    down_sum = dp_sum(home(down_own, down_away))
 
     proj_grads = [None] * groups
     qkv_grads = [None] * groups
@@ -328,35 +362,35 @@
     for at in reversed(range(len(stages))):
         stage = stages[at]
         cols = head_cols * len(stage)
+        grad_heads = contract(back_pair, proj_mats[at], 1, 1).astype(bf16)
+        grad_qkv = attend_back(qkv_rows[at], grad_heads, heads_lse[at])
+        if at == len(stages) - 1:
+            grad_qkv, up_own, up_away = hold((grad_qkv, up_grads[0], up_away))
+            up_sum = dp_sum(home(up_own, up_away))
         proj_grad = contract(heads_out[at], back_pair, 0, 0)
-        grad_heads = contract(back_pair, proj_mats[at], 1, 1).astype(bf16)
-        parts = attend_back(qkv_rows[at], grad_heads, heads_lse[at], cols)
-        grad_qkv = jnp.concatenate(parts, axis=1)
-        qkv_grad = contract(attn_pair, grad_qkv, 0, 0).reshape(D, 3, cols)
+        qkv_grad = contract(attn_pair, grad_qkv, 0, 0)
         terms = contract(grad_qkv, qkv_mats[at], 1, 1)
         attn_terms = terms if attn_terms is None else attn_terms + terms
-        sums = jnp.sum(grad_qkv.astype(f32), axis=0).reshape(3, cols)
+        sums = jnp.sum(grad_qkv.astype(f32), axis=0).reshape(cols // LANES, 3, LANES)
+        sums = sums.swapaxes(0, 1).reshape(3, cols)
+        if len(stage) > 1:
+            qkv_grad = qkv_grad.reshape(D, cols // LANES, 3, LANES).swapaxes(1, 2)
+            qkv_grad = qkv_grad.reshape(D, 3, cols)
         for place, shard in enumerate(stage):
             span = slice(place * head_cols, (place + 1) * head_cols)
             proj_grads[shard] = proj_grad[span]
-            qkv_grads[shard] = qkv_grad[:, :, span]
+            qkv_grads[shard] = qkv_grad if len(stage) == 1 else qkv_grad[:, :, span]
             qv_sums[shard] = jnp.concatenate([sums[0, span], sums[2, span]])
-    proj_home, up_sum = lax.optimization_barrier((send_home(proj_grads), up_sum))
-    qkv_home = send_home(qkv_grads)
-
-    proj_bias_part = tensor_sum(jnp.sum(grad_branch_attn.astype(f32), axis=0))
-    down_bias_part = tensor_sum(jnp.sum(grad_branch_mlp.astype(f32), axis=0))
-    small_own = [
-        jnp.concatenate([up_bias_sums[shard], qv_sums[shard]]) for shard in range(groups)
-    ]
-    small_home = small_own[0]
-    for step in range(1, groups):
-        small_home = small_home + group_move(small_own[step], -step)
-    small = jnp.concatenate([small_home, proj_bias_part, down_bias_part]).astype(bf16)
-
-    qkv_sum, proj_sum, small_sum = lax.psum((qkv_home, proj_home, small), "dp")
+    proj_away = away(proj_grads)
+    qkv_away = away(qkv_grads)
 
     grad_attn_input = pair_scatter(attn_terms)
+    grad_attn_input, qkv_away, proj_away = hold((grad_attn_input, qkv_away, proj_away))
+    proj_sum = dp_sum(home(proj_grads[0], proj_away))
+    qkv_sum = dp_sum(home(qkv_grads[0], qkv_away))
+    if qkv_sum.ndim == 2:
+        qkv_sum = qkv_sum.reshape(D, head_cols // LANES, 3, LANES).swapaxes(1, 2)
+        qkv_sum = qkv_sum.reshape(D, 3, head_cols)
     tokens_grad = grad_hidden_state + norm_back(
         grad_attn_input * (1.0 + scale_attn), normed_attn, inv_attn
     )
@@ -373,25 +407,48 @@
             )
         ]
     )
-    mod_whole = mod_sums
-    for step in range(1, pair):
-        mod_whole = mod_whole + pair_move(mod_sums, step)
-    share = 6 * D // pair
-    mod_share = lax.dynamic_slice_in_dim(
-        mod_whole.astype(bf16), (tensor_at % pair) * share, share, axis=0
-    )
-    mod_grads = lax.all_gather(mod_share[None], ("dp", "tensor"), axis=0, tiled=True)
-    mod_grads = mod_grads.reshape(dp_size * latents_local, 6 * D)
     ada_cols = ada_weight.shape[1]
-    mod_own = lax.dynamic_slice_in_dim(mod_grads, tensor_at * ada_cols, ada_cols, axis=1)
-    ada_weight_grad = contract(silu_all, mod_own, 0, 0)
-    ada_bias_grad = jnp.sum(mod_own.astype(f32), axis=0)
-    mod_here = lax.dynamic_slice_in_dim(mod_own, dp_at * latents_local, latents_local, axis=0)
-    silu_grad = tensor_sum(contract(mod_here, ada_weight, 1, 1))
+    mod_own = jnp.zeros((latents_local, ada_cols), f32)
+    latent_index = jnp.arange(latents_local, dtype=jnp.int32)[:, None]
+    for step in range(tensor_size):
+        target = (tensor_at + step) % tensor_size
+        piece = lax.dynamic_slice_in_dim(mod_sums, target * ada_cols, ada_cols, axis=0)
+        if step:
+            moves = [(i, (i + step) % tensor_size) for i in range(tensor_size)]
+            piece = lax.ppermute(piece, "tensor", moves)
+        source = (tensor_at + tensor_size - step) % tensor_size
+        mod_own = mod_own + jnp.where(latent_index == source // pair, piece[None], 0.0)
+    mod_own = mod_own.astype(bf16)
+    silu_grad = tensor_sum(contract(mod_own, ada_weight, 1, 1))
     condition_grad = silu_grad * (cond_sig * (1.0 + cond_wide * (1.0 - cond_sig)))
 
-    ff_local = up_weight.shape[0]
-    small_sum = small_sum.astype(f32)
+    bias_sums = tensor_sum(
+        jnp.stack(
+            [
+                jnp.sum(grad_branch_attn.astype(f32), axis=0),
+                jnp.sum(grad_branch_mlp.astype(f32), axis=0),
+            ]
+        )
+    )
+    small_own = [
+        jnp.concatenate([up_bias_sums[shard], qv_sums[shard]]) for shard in range(groups)
+    ]
+    small = small_own[0]
+    for step in range(1, groups):
+        small = small + group_move(small_own[step], -step)
+    small = jnp.concatenate([small, bias_sums.reshape(-1)])
+    small_size = small.shape[0]
+    pad = -small_size % (latents_local * LANES)
+    small = jnp.pad(small, (0, pad)).astype(bf16).reshape(latents_local, -1)
+    gathered = dp_gather(jnp.concatenate([silu_low, mod_own, small], axis=1))
+    silu_all = gathered[:, :D]
+    mod_all_own = gathered[:, D : D + ada_cols]
+    ada_weight_grad = contract(silu_all, mod_all_own, 0, 0)
+    ada_bias_grad = jnp.sum(mod_all_own.astype(f32), axis=0)
+    small_sum = jnp.sum(
+        gathered[:, D + ada_cols :].astype(f32).reshape(dp_size, -1), axis=0
+    )[:small_size]
+
     at_qv = ff_local
     at_proj = at_qv + 2 * head_cols
     return (

time: 586 us -> 767 us (1.31)
  waiting for transfers between devices: 220 us -> 459 us
  blocking collectives: 96.8 us -> 42.3 us
  matrix products: 114 us -> 94 us
  other arithmetic: 34.9 us -> 45 us
    reduce_scatter x0 -> x4, waiting for transfers between devices: none -> 213 us  [dp_sum(): part = lax.psum_scatter(values, 'dp', scatter_dimension=0, tiled=True)]
    psum x3 -> x0, waiting for transfers between devices: 106 us -> none  [the longest x1 91.7 us: shards(): up_sum = lax.psum(up_home, 'dp')]
    all_gather x2 -> x5, waiting for transfers between devices: 16.3 us -> 122 us  [the longest x3 98.5 us: dp_sum(): return lax.all_gather(part, 'dp', axis=0, tiled=True)]
    all_gather x2 -> x1, blocking collectives: 73.1 us -> 32.1 us  [dp_sum(): return lax.all_gather(part, 'dp', axis=0, tiled=True)]
    dot_general x18, matrix products: 85.2 us -> 64.9 us  [contract(): lax.dot_general(left, right, (((left_dim,), (right_dim,)), ((), ())), pre...]
    psum x1 -> x0, blocking collectives: 17.4 us -> none  [shards(): qkv_sum, proj_sum, small_sum = lax.psum((qkv_home, proj_home, small), 'dp')]
    ppermute x14 -> x12, waiting for transfers between devices: 93.4 us -> 107 us  [group_move(): return lax.ppermute(values, 'tensor', moves)]
    ppermute x0 -> x6, waiting for transfers between devices: none -> 11.3 us  [the longest x3 11.2 us: dp_gather(): rows = jnp.concatenate([rows, lax.ppermute(rows, 'dp', moves)], axis=0)]
  transfers between devices with their start and end apart: 31 -> 37, of which waited for: 12 -> 21; matrix products, arithmetic and copies ran while one was open for 28% -> 16% of each run, Pallas kernels for 9% -> 7%
where the time goes in v2:
time: 767 us; the launch traced here: 757 us
  waiting for transfers between devices  459 us (60%)
  matrix products  94 us (12%)
  Pallas kernels  52.5 us (7%)
  other arithmetic  45 us (6%)
  blocking collectives  42.3 us (6%)
  local copies, waits for them, and re-layouts  25.9 us (3%)
  starting transfers between devices  22.9 us (3%)
  between operations  15 us (2%)
    reduce_scatter x4, waiting for transfers between devices, dp_sum(): part = lax.psum_scatter(values, 'dp', scatter_dimension=0, tiled=True)  213 us
    ppermute x12, waiting for transfers between devices, group_move(): return lax.ppermute(values, 'tensor', moves)  107 us
    all_gather x3, waiting for transfers between devices, dp_sum(): return lax.all_gather(part, 'dp', axis=0, tiled=True)  98.5 us
    dot_general x18, matrix products, contract(): lax.dot_general(left, right, (((left_dim,), (right_dim,)), ((), ())), pre...  64.9 us
    all_gather x1, blocking collectives, dp_sum(): return lax.all_gather(part, 'dp', axis=0, tiled=True)  32.1 us
    pallas_call x2, Pallas kernels, attend_back(): pl.pallas_call(attend_back_kernel, grid=(blocks,), in_specs=[column_spec(...  31.8 us
    all_gather x2, waiting for transfers between devices, spread_gather(): return [lax.all_gather(piece, 'dp', axis=0, tiled=True) for piece in pieces]  23.3 us
    pallas_call x2, Pallas kernels, attend(): pl.pallas_call(attend_kernel, grid=(blocks,), in_specs=[column_spec(3 * L...  20.8 us
  transfers between devices with their start and end apart: 37, of which 21 were waited for; matrix products, arithmetic and copies ran while one was open for 16% of the time, Pallas kernels for 7%

profile of v2, /device:TPU:0, one launch (start us, length us, event | category | flops | bytes accessed | tf_op | source)
XLA Modules:
  0.0 756.8 jit_solution(13640499953104410324)
XLA Ops:
  15.0 10.2 %all_gather.21 = bf16[2,6144]{1,0:T(2,128)(2,1)S(1)} all-gather(bf16[2,1536]{1,0:T(2,128)(2,1)S(1)} %fusion.20), channel_id=1, replica_groups=mesh['dp'=8,'tensor'=4] {'tensor'}, dimensions={1}, use_global_device_ids=true | all-gather | bytes 30720 | tf_op jit(solution)/shard_map/all_gather | solution.py:269
  40.5 33.6 %collective-permute-done.5 = bf16[1536]{0:T(1024)(128)(2,1)S(1)} collective-permute-done((bf16[1536]{0:T(1024)(128)(2,1)S(1)}, bf16[1536]{0:T(1024)(128)(2,1)S(1)}, u32[]{:S(2)}, u32[]{:S(2)}) %collective-permute-start.5) | collective-permute-done | bytes 3104 | tf_op jit(solution)/shard_map/ppermute | solution.py:185
  76.9 5.2 add_convert_fusion.4.qkv_ref
  82.0 10.2 %attend.2 = (bf16[1024,256]{1,0:T(8,128)(2,1)}, f32[2,2,1024]{2,1,0:T(2,128)}) custom-call(bf16[1024,768]{1,0:T(8,128)(2,1)} %add_convert_fusion.4.qkv_ref), custom_call_target="tpu_custom_call" | custom-call | tf_op jit(solution)/shard_map/attend/pallas_call | solution.py:125
  92.3 4.4 add_convert_fusion.3.qkv_ref
  96.7 10.5 %attend.3 = (bf16[1024,256]{1,0:T(8,128)(2,1)}, f32[2,2,1024]{2,1,0:T(2,128)}) custom-call(bf16[1024,768]{1,0:T(8,128)(2,1)} %add_convert_fusion.3.qkv_ref), custom_call_target="tpu_custom_call" | custom-call | tf_op jit(solution)/shard_map/attend/pallas_call | solution.py:125
  107.2 23.3 %all-gather.8.cloned.1.call-done = bf16[1024,1024]{1,0:T(8,128)(2,1)} async-done(((bf16[128,1024]{1,0:T(8,128)(2,1)}), bf16[1024,1024]{1,0:T(8,128)(2,1)}) %all-gather.8.cloned.1.call-update) | async-done | bytes 2097168 | tf_op jit(solution)/shard_map/all_gather | solution.py:215
  144.2 4.8 fusion.66
  149.0 6.3 convert_reduce_fusion.1
  160.1 6.5 convert_reduce_fusion
  169.3 5.1 convolution_add_fusion.4
  175.0 5.3 convolution_convert_fusion.1
  190.7 4.4 fusion.62
  195.2 5.1 fusion.59
  200.5 28.3 %collective-permute-done.12 = bf16[1024,1024]{1,0:T(8,128)(2,1)S(1)} collective-permute-done((bf16[1024,1024]{1,0:T(8,128)(2,1)S(1)}, bf16[1024,1024]{1,0:T(8,128)(2,1)S(1)}, u32[]{:S(2)}, u32[]{:S(2)}) %collective-permute-start.12) | collective-permute-done | bytes 2097184 | tf_op jit(solution)/shard_map/ppermute | solution.py:185
  231.8 16.0 %attend_back.2 = bf16[1024,768]{1,0:T(8,128)(2,1)} custom-call(bf16[1024,768]{1,0:T(8,128)(2,1)} %add_convert_fusion.3.qkv_ref, bf16[1024,256]{1,0:T(8,128)(2,1)} %convolution_convert_fusion.5.do_ref, f32[2,2,1024]{2,1,0:T(2,128)} %get-tuple-element.47.lse_ref), custom_call_target="tpu_custom_call" | custom-call | tf_op jit(solution)/shard_map/attend_back/pallas_call | solution.py:141
  250.5 22.5 %collective-permute-done.13 = bf16[1024,1024]{1,0:T(8,128)(2,1)} collective-permute-done((bf16[1024,1024]{1,0:T(8,128)(2,1)}, bf16[1024,1024]{1,0:T(8,128)(2,1)}, u32[]{:S(2)}, u32[]{:S(2)}) %collective-permute-start.13) | collective-permute-done | bytes 2097184 | tf_op jit(solution)/shard_map/ppermute | solution.py:185
  277.6 15.8 %attend_back.3 = bf16[1024,768]{1,0:T(8,128)(2,1)} custom-call(bf16[1024,768]{1,0:T(8,128)(2,1)} %add_convert_fusion.4.qkv_ref, bf16[1024,256]{1,0:T(8,128)(2,1)} %convolution_convert_fusion.4.do_ref, f32[2,2,1024]{2,1,0:T(2,128)} %get-tuple-element.49.lse_ref), custom_call_target="tpu_custom_call" | custom-call | tf_op jit(solution)/shard_map/attend_back/pallas_call | solution.py:141
  304.8 18.4 %collective-permute-done.16 = bf16[256,1024]{1,0:T(8,128)(2,1)} collective-permute-done((bf16[256,1024]{1,0:T(8,128)(2,1)S(1)}, bf16[256,1024]{1,0:T(8,128)(2,1)}, u32[]{:S(2)}, u32[]{:S(2)}) %collective-permute-start.16) | collective-permute-done | bytes 524320 | tf_op jit(solution)/shard_map/ppermute | solution.py:185
  323.2 4.5 add_convert_fusion.2
  327.8 5.0 add_convert_fusion
  332.9 5.0 add_convert_fusion.1
  341.4 50.8 %reduce-scatter.5.cloned.1.call-done = bf16[128,768]{1,0:T(8,128)(2,1)} async-done(((bf16[1024,768]{1,0:T(8,128)(2,1)}), bf16[128,768]{1,0:T(8,128)(2,1)}) %reduce-scatter.5.cloned.1.call-update) | async-done | bytes 196624 | tf_op jit(solution)/shard_map/reduce_scatter | solution.py:227
  392.5 70.3 %reduce-scatter.11.cloned.1.call-done = bf16[128,1024]{1,0:T(8,128)(2,1)} async-done(((bf16[1024,1024]{1,0:T(8,128)(2,1)}), bf16[128,1024]{1,0:T(8,128)(2,1)}) %reduce-scatter.11.cloned.1.call-update) | async-done | bytes 262160 | tf_op jit(solution)/shard_map/reduce_scatter | solution.py:227
  474.9 4.1 multiply_reduce_fusion.1
  481.1 52.9 %reduce-scatter.9.cloned.1.call-done = bf16[128,1024]{1,0:T(8,128)(2,1)} async-done(((bf16[1024,1024]{1,0:T(8,128)(2,1)}), bf16[128,1024]{1,0:T(8,128)(2,1)}) %reduce-scatter.9.cloned.1.call-update) | async-done | bytes 262160 | tf_op jit(solution)/shard_map/reduce_scatter | solution.py:227
  549.9 5.0 collective-permute-done.27
  560.6 38.9 %reduce-scatter.7.cloned.1.call-done = bf16[32,1024]{1,0:T(8,128)(2,1)} async-done(((bf16[256,1024]{1,0:T(8,128)(2,1)}), bf16[32,1024]{1,0:T(8,128)(2,1)}) %reduce-scatter.7.cloned.1.call-update) | async-done | bytes 65552 | tf_op jit(solution)/shard_map/reduce_scatter | solution.py:227
  599.5 32.1 %all_gather.25 = bf16[256,1024]{1,0:T(8,128)(2,1)S(1)} all-gather(bf16[32,1024]{1,0:T(8,128)(2,1)} %reduce-scatter.7.cloned.1.call-done), channel_id=1, replica_groups=mesh['dp'=8,'tensor'=4] {'dp'}, dimensions={0}, use_global_device_ids=true | all-gather | bytes 589824 | tf_op jit(solution)/shard_map/all_gather | solution.py:228
  632.7 13.3 %all-gather.10.cloned.1.call-done = bf16[1024,768]{1,0:T(8,128)(2,1)} async-done(((bf16[128,768]{1,0:T(8,128)(2,1)}), bf16[1024,768]{1,0:T(8,128)(2,1)}) %all-gather.10.cloned.1.call-update) | async-done | bytes 1572880 | tf_op jit(solution)/shard_map/all_gather | solution.py:228
  656.7 39.5 %all-gather.14.cloned.1.call-done = bf16[1024,1024]{1,0:T(8,128)(2,1)} async-done(((bf16[128,1024]{1,0:T(8,128)(2,1)}), bf16[1024,1024]{1,0:T(8,128)(2,1)}) %all-gather.14.cloned.1.call-update) | async-done | bytes 2097168 | tf_op jit(solution)/shard_map/all_gather | solution.py:228
  700.2 45.7 %all-gather.12.cloned.1.call-done = bf16[1024,1024]{1,0:T(8,128)(2,1)} async-done(((bf16[128,1024]{1,0:T(8,128)(2,1)}), bf16[1024,1024]{1,0:T(8,128)(2,1)}) %all-gather.12.cloned.1.call-update) | async-done | bytes 2097168 | tf_op jit(solution)/shard_map/all_gather | solution.py:228
  (233 shorter events, 138.7 us)
Async XLA Ops:
  7.2 100.0 %all-gather.6.cloned.1.call-start = ((), (), s32[]{:S(2)}) async-start(), calls=%async_computation.4 | async-start | bytes 2359296 | tf_op jit(solution)/shard_map/all_gather | solution.py:215
  9.1 20.8 %collective-permute-start = (bf16[128,1024]{1,0:T(8,128)(2,1)}, bf16[128,1024]{1,0:T(8,128)(2,1)}, u32[]{:S(2)}, u32[]{:S(2)}) collective-permute-start(bf16[128,1024]{1,0:T(8,128)(2,1)} %constant_dynamic-slice_fusion.1), channel_id=1, source_target_pairs={{0,2},{1,3},{2,0},{3,1},{4,6},{5,7},{6,4},{7,5},{8,10},{9,11},{10,... | collective-permute-start | bytes 786440 | tf_op jit(solution)/shard_map/ppermute | solution.py:185
  13.0 16.9 %collective-permute-start.1 = (bf16[128,1024]{1,0:T(8,128)(2,1)S(1)}, bf16[128,1024]{1,0:T(8,128)(2,1)}, u32[]{:S(2)}, u32[]{:S(2)}) collective-permute-start(bf16[128,1024]{1,0:T(8,128)(2,1)S(1)} %constant_dynamic-slice_fusion), channel_id=1, source_target_pairs={{0,2},{1,3},{2,0},{3,1},{4,6},{5,7},{6,4},{7,5},{8,10},{9,11},{10,... | collective-permute-start | bytes 786440 | tf_op jit(solution)/shard_map/ppermute | solution.py:185
  29.9 100.6 %all-gather.8.cloned.1.call-start = ((), (), s32[]{:S(2)}) async-start(), calls=%async_computation.5 | async-start | bytes 2359296 | tf_op jit(solution)/shard_map/all_gather | solution.py:215
  30.7 361.5 %reduce-scatter.5.cloned.1.call-start = ((), (), s32[]{:S(2)}) async-start(), calls=%async_computation.6 | async-start | bytes 1769472 | tf_op jit(solution)/shard_map/reduce_scatter | solution.py:227
  30.7 44.8 %collective-permute-start.2 = (bf16[512,1024]{1,0:T(8,128)(2,1)}, bf16[512,1024]{1,0:T(8,128)(2,1)}, u32[]{:S(2)}, u32[]{:S(2)}) collective-permute-start(bf16[512,1024]{1,0:T(8,128)(2,1)} %fusion.22), channel_id=1, source_target_pairs={{0,1},{1,0},{2,3},{3,2},{4,5},{5,4},{6,7},{7,6},{8,9},{9,8},{10,11... | collective-permute-start | bytes 3145736 | tf_op jit(solution)/shard_map/ppermute | solution.py:181
  36.6 55.7 %collective-permute-start.3 = (bf16[1024,768]{0,1:T(8,128)(2,1)}, bf16[1024,768]{0,1:T(8,128)(2,1)}, u32[]{:S(2)}, u32[]{:S(2)}) collective-permute-start(bf16[1024,768]{0,1:T(8,128)(2,1)} %bitcast.5), channel_id=1, source_target_pairs={{0,2},{1,3},{2,0},{3,1},{4,6},{5,7},{6,4},{7,5},{8,10},{9,11},{10,... | collective-permute-start | bytes 4718600 | tf_op jit(solution)/shard_map/ppermute | solution.py:185
  38.3 35.8 %collective-permute-start.5 = (bf16[1536]{0:T(1024)(128)(2,1)S(1)}, bf16[1536]{0:T(1024)(128)(2,1)S(1)}, u32[]{:S(2)}, u32[]{:S(2)}) collective-permute-start(bf16[1536]{0:T(1024)(128)(2,1)S(1)} %constant_dynamic-update-slice_fusion.4), channel_id=1, source_target_pairs={{0,2},{1,3},{2,0},{3,1},{4,6},{5,7},{6,4},{7,5},{8,10},{9,11},{10,... | collective-permute-start | bytes 9224 | tf_op jit(solution)/shard_map/ppermute | solution.py:185
  38.7 53.6 %collective-permute-start.4 = (bf16[256,1024]{1,0:T(8,128)(2,1)}, bf16[256,1024]{1,0:T(8,128)(2,1)}, u32[]{:S(2)}, u32[]{:S(2)}) collective-permute-start(bf16[256,1024]{1,0:T(8,128)(2,1)} %param.19), channel_id=1, source_target_pairs={{0,2},{1,3},{2,0},{3,1},{4,6},{5,7},{6,4},{7,5},{8,10},{9,11},{10,... | collective-permute-start | bytes 1572872 | tf_op jit(solution)/shard_map/ppermute | solution.py:185
  140.2 8.8 %collective-permute-start.9 = (bf16[512,1024]{1,0:T(8,128)(2,1)S(1)}, bf16[512,1024]{1,0:T(8,128)(2,1)S(1)}, u32[]{:S(2)}, u32[]{:S(2)}) collective-permute-start(bf16[512,1024]{1,0:T(8,128)(2,1)S(1)} %get-tuple-element.97), channel_id=1, source_target_pairs={{0,1},{1,0},{2,3},{3,2},{4,5},{5,4},{6,7},{7,6},{8,9},{9,8},{10,11... | collective-permute-start | bytes 3145736 | tf_op jit(solution)/shard_map/ppermute | solution.py:181
  169.1 17.0 %collective-permute-start.10 = (bf16[512,1024]{1,0:T(8,128)(2,1)S(1)}, bf16[512,1024]{1,0:T(8,128)(2,1)S(1)}, u32[]{:S(2)}, u32[]{:S(2)}) collective-permute-start(bf16[512,1024]{1,0:T(8,128)(2,1)S(1)} %slice.225), channel_id=1, source_target_pairs={{0,1},{1,0},{2,3},{3,2},{4,5},{5,4},{6,7},{7,6},{8,9},{9,8},{10,11... | collective-permute-start | bytes 3145736 | tf_op jit(solution)/shard_map/ppermute | solution.py:181
  174.6 12.6 %collective-permute-start.8 = (bf16[512,1024]{1,0:T(8,128)(2,1)S(1)}, bf16[512,1024]{1,0:T(8,128)(2,1)S(1)}, u32[]{:S(2)}, u32[]{:S(2)}) collective-permute-start(bf16[512,1024]{1,0:T(8,128)(2,1)S(1)} %slice.226), channel_id=1, source_target_pairs={{0,1},{1,0},{2,3},{3,2},{4,5},{5,4},{6,7},{7,6},{8,9},{9,8},{10,11... | collective-permute-start | bytes 3145736 | tf_op jit(solution)/shard_map/ppermute | solution.py:181
  180.3 48.6 %collective-permute-start.12 = (bf16[1024,1024]{1,0:T(8,128)(2,1)S(1)}, bf16[1024,1024]{1,0:T(8,128)(2,1)S(1)}, u32[]{:S(2)}, u32[]{:S(2)}) collective-permute-start(bf16[1024,1024]{1,0:T(8,128)(2,1)S(1)} %convolution_convert_fusion.1), channel_id=1, source_target_pairs={{0,2},{1,3},{2,0},{3,1},{4,6},{5,7},{6,4},{7,5},{8,10},{9,11},{10,... | collective-permute-start | bytes 6291464 | tf_op jit(solution)/shard_map/ppermute | solution.py:185
  185.6 87.4 %collective-permute-start.13 = (bf16[1024,1024]{1,0:T(8,128)(2,1)}, bf16[1024,1024]{1,0:T(8,128)(2,1)}, u32[]{:S(2)}, u32[]{:S(2)}) collective-permute-start(bf16[1024,1024]{1,0:T(8,128)(2,1)} %convolution_convert_fusion), channel_id=1, source_target_pairs={{0,2},{1,3},{2,0},{3,1},{4,6},{5,7},{6,4},{7,5},{8,10},{9,11},{10,... | collective-permute-start | bytes 6291464 | tf_op jit(solution)/shard_map/ppermute | solution.py:185
  190.6 9.6 %collective-permute-start.11 = (bf16[512,1024]{1,0:T(8,128)(2,1)S(1)}, bf16[512,1024]{1,0:T(8,128)(2,1)S(1)}, u32[]{:S(2)}, u32[]{:S(2)}) collective-permute-start(bf16[512,1024]{1,0:T(8,128)(2,1)S(1)} %get-tuple-element.103), channel_id=1, source_target_pairs={{0,1},{1,0},{2,3},{3,2},{4,5},{5,4},{6,7},{7,6},{8,9},{9,8},{10,11... | collective-permute-start | bytes 3145736 | tf_op jit(solution)/shard_map/ppermute | solution.py:181
  276.1 47.1 %collective-permute-start.15 = (bf16[1024,768]{1,0:T(8,128)(2,1)}, bf16[1024,768]{1,0:T(8,128)(2,1)}, u32[]{:S(2)}, u32[]{:S(2)}) collective-permute-start(bf16[1024,768]{1,0:T(8,128)(2,1)} %convolution_convert_fusion.2), channel_id=1, source_target_pairs={{0,2},{1,3},{2,0},{3,1},{4,6},{5,7},{6,4},{7,5},{8,10},{9,11},{10,... | collective-permute-start | bytes 4718600 | tf_op jit(solution)/shard_map/ppermute | solution.py:185
  302.1 21.1 %collective-permute-start.16 = (bf16[256,1024]{1,0:T(8,128)(2,1)S(1)}, bf16[256,1024]{1,0:T(8,128)(2,1)}, u32[]{:S(2)}, u32[]{:S(2)}) collective-permute-start(bf16[256,1024]{1,0:T(8,128)(2,1)S(1)} %convolution_convert_fusion.3), channel_id=1, source_target_pairs={{0,2},{1,3},{2,0},{3,1},{4,6},{5,7},{6,4},{7,5},{8,10},{9,11},{10,... | collective-permute-start | bytes 1572872 | tf_op jit(solution)/shard_map/ppermute | solution.py:185
  327.8 135.0 %reduce-scatter.11.cloned.1.call-start = ((), (), s32[]{:S(2)}) async-start(), calls=%async_computation.11 | async-start | bytes 2359296 | tf_op jit(solution)/shard_map/reduce_scatter | solution.py:227
  332.8 201.2 %reduce-scatter.9.cloned.1.call-start = ((), (), s32[]{:S(2)}) async-start(), calls=%async_computation.9 | async-start | bytes 2359296 | tf_op jit(solution)/shard_map/reduce_scatter | solution.py:227
  337.9 261.6 %reduce-scatter.7.cloned.1.call-start = ((), (), s32[]{:S(2)}) async-start(), calls=%async_computation.8 | async-start | bytes 589824 | tf_op jit(solution)/shard_map/reduce_scatter | solution.py:227
  341.4 304.7 %all-gather.10.cloned.1.call-start = ((), (), s32[]{:S(2)}) async-start(), calls=%async_computation.7 | async-start | bytes 1769472 | tf_op jit(solution)/shard_map/all_gather | solution.py:228
  392.2 303.9 %all-gather.14.cloned.1.call-start = ((), (), s32[]{:S(2)}) async-start(), calls=%async_computation.12 | async-start | bytes 2359296 | tf_op jit(solution)/shard_map/all_gather | solution.py:228
  392.4 70.5 %collective-permute-start.23 = (f32[2,1024]{1,0:T(2,128)S(1)}, f32[2,1024]{1,0:T(2,128)S(1)}, u32[]{:S(2)}, u32[]{:S(2)}) collective-permute-start(f32[2,1024]{1,0:T(2,128)S(1)} %pad_maximum_fusion.13), channel_id=1, source_target_pairs={{0,1},{1,0},{2,3},{3,2},{4,5},{5,4},{6,7},{7,6},{8,9},{9,8},{10,11... | collective-permute-start | bytes 24584 | tf_op jit(solution)/shard_map/ppermute | solution.py:181
  462.8 283.2 %all-gather.12.cloned.1.call-start = ((), (), s32[]{:S(2)}) async-start(), calls=%async_computation.10 | async-start | bytes 2359296 | tf_op jit(solution)/shard_map/all_gather | solution.py:228
  462.9 3.7 collective-permute-start.24
  468.4 66.7 %collective-permute-start.22 = (f32[1536]{0:T(1024)S(1)}, f32[1536]{0:T(1024)S(1)}, u32[]{:S(2)}, u32[]{:S(2)}) collective-permute-start(f32[1536]{0:T(1024)S(1)} %pad_maximum_fusion.12), channel_id=1, source_target_pairs={{0,2},{1,3},{2,0},{3,1},{4,6},{5,7},{6,4},{7,5},{8,10},{9,11},{10,... | collective-permute-start | bytes 18440 | tf_op jit(solution)/shard_map/ppermute | solution.py:185
  479.2 54.9 %collective-permute-start.17 = (f32[1536]{0:T(1024)S(1)}, f32[1536]{0:T(1024)S(1)}, u32[]{:S(2)}, u32[]{:S(2)}) collective-permute-start(f32[1536]{0:T(1024)S(1)} %get-tuple-element.110), channel_id=1, source_target_pairs={{0,1},{1,2},{2,3},{3,0},{4,5},{5,6},{6,7},{7,4},{8,9},{9,10},{10,1... | collective-permute-start | bytes 18440 | tf_op jit(solution)/shard_map/ppermute | solution.py:418
  479.2 54.9 %collective-permute-start.18 = (f32[1536]{0:T(1024)S(1)}, f32[1536]{0:T(1024)S(1)}, u32[]{:S(2)}, u32[]{:S(2)}) collective-permute-start(f32[1536]{0:T(1024)S(1)} %get-tuple-element.109), channel_id=1, source_target_pairs={{0,2},{1,3},{2,0},{3,1},{4,6},{5,7},{6,4},{7,5},{8,10},{9,11},{10,... | collective-permute-start | bytes 18440 | tf_op jit(solution)/shard_map/ppermute | solution.py:418
  479.6 54.5 %collective-permute-start.19 = (f32[1536]{0:T(1024)S(1)}, f32[1536]{0:T(1024)S(1)}, u32[]{:S(2)}, u32[]{:S(2)}) collective-permute-start(f32[1536]{0:T(1024)S(1)} %get-tuple-element.108), channel_id=1, source_target_pairs={{0,3},{1,0},{2,1},{3,2},{4,7},{5,4},{6,5},{7,6},{8,11},{9,8},{10,9... | collective-permute-start | bytes 18440 | tf_op jit(solution)/shard_map/ppermute | solution.py:418
  540.6 3.8 collective-permute-start.25
  544.4 4.0 collective-permute-start.26
  548.5 6.4 collective-permute-start.27
  (34 other events, 355.0 us)
Sparse Core Ops, SparseCore 0:
  30.0 50.5 all-gather.5
  82.8 47.7 all-gather.7
  327.9 64.3 reduce-scatter.4
  395.6 67.0 reduce-scatter.10
  466.7 67.3 reduce-scatter.8
  537.8 61.6 reduce-scatter.6
  601.7 44.2 all-gather.9
  648.2 47.9 all-gather.13
  698.3 47.6 all-gather.11

commit v3 on v2

--- a/solution.py
+++ b/solution.py
@@ -206,9 +206,13 @@
     def fetch_direct(weight):
         return [weight] + [group_move(weight, step) for step in range(1, groups)]
 
-    def spread_pieces(weight):
-        piece_rows = weight.shape[0] // dp_size
-        piece = lax.dynamic_slice_in_dim(weight, dp_at * piece_rows, piece_rows, axis=0)
+    def spread_pieces(weights):
+        piece_rows = weights[0].shape[0] // dp_size
+        pieces = [
+            lax.dynamic_slice_in_dim(weight, dp_at * piece_rows, piece_rows, axis=0)
+            for weight in weights
+        ]
+        piece = jnp.concatenate(pieces, axis=1)
         return [group_move(piece, step) for step in range(1, groups)]
 
     def spread_gather(pieces):
@@ -223,16 +227,31 @@
             total = total + piece.astype(f32)
         return total.astype(bf16)
 
-    def dp_sum(values):
-        part = lax.psum_scatter(values, "dp", scatter_dimension=0, tiled=True)
-        return lax.all_gather(part, "dp", axis=0, tiled=True)
+    def dp_move(values, bit):
+        return lax.ppermute(values, "dp", [(i, i ^ bit) for i in range(dp_size)])
+
+    bits = [1 << at for at in range(dp_size.bit_length() - 1)]
+    turned = bits[1:] + bits[:1]
+
+    def dp_sum(values, order):
+        part = values
+        for bit in order:
+            half = part.shape[0] // 2
+            mine = (dp_at // bit) % 2
+            keep = lax.dynamic_slice_in_dim(part, mine * half, half, axis=0)
+            give = lax.dynamic_slice_in_dim(part, (1 - mine) * half, half, axis=0)
+            part = (keep.astype(f32) + dp_move(give, bit).astype(f32)).astype(bf16)
+        for bit in reversed(order):
+            first = (dp_at // bit) % 2 == 0
+            other = dp_move(part, bit)
+            part = jnp.concatenate(
+                [jnp.where(first, part, other), jnp.where(first, other, part)], axis=0
+            )
+        return part
 
     def dp_gather(rows):
-        step = 1
-        while step < dp_size:
-            moves = [(i, i ^ step) for i in range(dp_size)]
-            rows = jnp.concatenate([rows, lax.ppermute(rows, "dp", moves)], axis=0)
-            step *= 2
+        for bit in bits:
+            rows = jnp.concatenate([rows, dp_move(rows, bit)], axis=0)
         return rows
 
     hold = lax.optimization_barrier
@@ -250,15 +269,13 @@
     if head_cols % LANES == 0:
         blocks = head_cols // LANES
         qkv_flat = qkv_weight.reshape(D, 3, blocks, LANES).swapaxes(1, 2).reshape(D, 3 * head_cols)
+        condition, qkv_flat = hold((condition, qkv_flat))
         qkv_of = fetch_direct(qkv_flat)
     else:
         qkv_of = fetch_direct(qkv_weight)
     proj_of = fetch_direct(proj_weight)
     small_of = fetch_direct(jnp.concatenate([up_bias, qv_bias.reshape(-1)]))
-    qv_bias_of = [part[ff_local:].reshape(2, head_cols) for part in small_of]
-    up_bias_of = [part[:ff_local] for part in small_of]
-    up_pieces = spread_pieces(up_weight)
-    down_pieces = spread_pieces(down_weight)
+    far_pieces = spread_pieces([up_weight, down_weight])
 
     cond_wide = condition.astype(f32)
     cond_sig = jax.nn.sigmoid(cond_wide)
@@ -276,9 +293,8 @@
     grad_wide = out_grad.astype(f32)
     normed_attn, inv_attn = layer_norm(tokens_wide)
     attn_input = (normed_attn * (1.0 + scale_attn) + shift_attn).astype(bf16)
-    attn_input, up_pieces, down_pieces = hold((attn_input, up_pieces, down_pieces))
-    up_far = spread_gather(up_pieces)
-    down_far = spread_gather(down_pieces)
+    attn_input, far_pieces = hold((attn_input, far_pieces))
+    far = spread_gather(far_pieces)
     attn_pair = pair_gather(attn_input)
     grad_branch_mlp = (gate_mlp * grad_wide).astype(bf16)
 
@@ -286,7 +302,8 @@
     proj_terms = None
     for at, stage in enumerate(stages):
         cols = head_cols * len(stage)
-        bias = joined([qv_bias_of[s] for s in stage], 1)
+        bias = [small_of[s][ff_local:].reshape(2, head_cols) if s else qv_bias for s in stage]
+        bias = joined(bias, 1)
         shift = jnp.stack([bias[0], jnp.zeros_like(bias[0]), bias[1]]).astype(f32)
         shift = shift.reshape(3, cols // LANES, LANES).swapaxes(0, 1).reshape(3 * cols)
         if head_cols % LANES == 0:
@@ -298,11 +315,11 @@
         rows = (jnp.dot(attn_pair, weight, preferred_element_type=f32) + shift).astype(bf16)
         heads, lse = attend(rows)
         if at == 0 and len(stages) > 1:
-            heads, qkv_of[1:], proj_of[1:], small_of = hold(
-                (heads, qkv_of[1:], proj_of[1:], small_of)
+            heads, qkv_of[1:], proj_of[1:], small_of[1:] = hold(
+                (heads, qkv_of[1:], proj_of[1:], small_of[1:])
             )
         if at == len(stages) - 1:
-            heads, up_far, down_far = hold((heads, up_far, down_far))
+            heads, far = hold((heads, far))
         proj = joined([proj_of[s] for s in stage], 0)
         terms = jnp.dot(heads, proj, preferred_element_type=f32)
         proj_terms = terms if proj_terms is None else proj_terms + terms
@@ -311,8 +328,9 @@
         heads_out.append(heads)
         heads_lse.append(lse)
         proj_mats.append(proj)
-    up_of = [up_weight] + list(up_far)
-    down_of = [down_weight] + list(down_far)
+    up_of = [up_weight] + [part[:, :D] for part in far]
+    down_of = [down_weight] + [part[:, D:] for part in far]
+    up_bias_of = [up_bias] + [part[:ff_local] for part in small_of[1:]]
     grad_pair = pair_gather(grad_branch_mlp)
     branch_attn = pair_scatter(proj_terms) + proj_bias.astype(f32)
     hidden_state = tokens_wide + gate_attn * branch_attn
@@ -352,8 +370,6 @@
     )
     grad_branch_attn = (gate_attn * grad_hidden_state).astype(bf16)
     back_pair = pair_gather(grad_branch_attn)
-    back_pair, down_own, down_away = hold((back_pair, down_grads[0], down_away))
-    down_sum = dp_sum(home(down_own, down_away))
 
     proj_grads = [None] * groups
     qkv_grads = [None] * groups
@@ -365,9 +381,12 @@
         grad_heads = contract(back_pair, proj_mats[at], 1, 1).astype(bf16)
         grad_qkv = attend_back(qkv_rows[at], grad_heads, heads_lse[at])
         if at == len(stages) - 1:
+            grad_qkv, down_own, down_away = hold((grad_qkv, down_grads[0], down_away))
+            down_sum = dp_sum(home(down_own, down_away), bits)
+        if at == 0:
             grad_qkv, up_own, up_away = hold((grad_qkv, up_grads[0], up_away))
-            up_sum = dp_sum(home(up_own, up_away))
-        proj_grad = contract(heads_out[at], back_pair, 0, 0)
+            up_sum = dp_sum(home(up_own, up_away), turned)
+        proj_grad = contract(back_pair, heads_out[at], 0, 0)
         qkv_grad = contract(attn_pair, grad_qkv, 0, 0)
         terms = contract(grad_qkv, qkv_mats[at], 1, 1)
         attn_terms = terms if attn_terms is None else attn_terms + terms
@@ -378,17 +397,27 @@
             qkv_grad = qkv_grad.reshape(D, 3, cols)
         for place, shard in enumerate(stage):
             span = slice(place * head_cols, (place + 1) * head_cols)
-            proj_grads[shard] = proj_grad[span]
-            qkv_grads[shard] = qkv_grad if len(stage) == 1 else qkv_grad[:, :, span]
+            proj_grads[shard] = proj_grad[:, span]
+            part = qkv_grad if len(stage) == 1 else qkv_grad[:, :, span].reshape(D, -1)
+            qkv_grads[shard] = part
             qv_sums[shard] = jnp.concatenate([sums[0, span], sums[2, span]])
     proj_away = away(proj_grads)
     qkv_away = away(qkv_grads)
 
     grad_attn_input = pair_scatter(attn_terms)
     grad_attn_input, qkv_away, proj_away = hold((grad_attn_input, qkv_away, proj_away))
-    proj_sum = dp_sum(home(proj_grads[0], proj_away))
-    qkv_sum = dp_sum(home(qkv_grads[0], qkv_away))
-    if qkv_sum.ndim == 2:
+    attn_home = jnp.concatenate(
+        [home(qkv_grads[0], qkv_away), home(proj_grads[0], proj_away)], axis=1
+    )
+    middle = attn_home.shape[1] // 2
+    attn_sum = jnp.concatenate(
+        [dp_sum(attn_home[:, :middle], bits), dp_sum(attn_home[:, middle:], turned)], axis=1
+    )
+    qkv_sum = attn_sum[:, : 3 * head_cols]
+    proj_sum = attn_sum[:, 3 * head_cols :].T
+    if len(stages[0]) > 1:
+        qkv_sum = qkv_sum.reshape(D, 3, head_cols)
+    else:
         qkv_sum = qkv_sum.reshape(D, head_cols // LANES, 3, LANES).swapaxes(1, 2)
         qkv_sum = qkv_sum.reshape(D, 3, head_cols)
     tokens_grad = grad_hidden_state + norm_back(

time: 767 us -> 551 us (0.72)
  waiting for transfers between devices: 459 us -> 226 us
  blocking collectives: 42.3 us -> 7.2 us
  starting transfers between devices: 22.9 us -> 44.8 us
  local copies, waits for them, and re-layouts: 25.9 us -> 39.8 us
  other arithmetic: 45 us -> 56.2 us
    reduce_scatter x4 -> x0, waiting for transfers between devices: 213 us -> none  [dp_sum(): part = lax.psum_scatter(values, 'dp', scatter_dimension=0, tiled=True)]
    all_gather x3 -> x0, waiting for transfers between devices: 98.5 us -> none  [dp_sum(): return lax.all_gather(part, 'dp', axis=0, tiled=True)]
    ppermute x3 -> x27, waiting for transfers between devices: 11.2 us -> 96 us  [dp_move(): return lax.ppermute(values, 'dp', [(i, i ^ bit) for i in range(dp_size)])]
    all_gather x1 -> x0, blocking collectives: 32.1 us -> none  [dp_sum(): return lax.all_gather(part, 'dp', axis=0, tiled=True)]
    ppermute x3 -> x27, starting transfers between devices: 3 us -> 25.9 us  [dp_move(): return lax.ppermute(values, 'dp', [(i, i ^ bit) for i in range(dp_size)])]
    all_gather x2 -> x1, waiting for transfers between devices: 23.3 us -> 10.2 us  [spread_gather(): return [lax.all_gather(piece, 'dp', axis=0, tiled=True) for piece in pieces]]
    convert_element_type x0 -> x13, other arithmetic: none -> 11 us  [the longest x12 9.09 us: dp_sum(): part = (keep.astype(f32) + dp_move(give, bit).astype(f32)).astype(bf16)]
    ppermute x12 -> x11, waiting for transfers between devices: 107 us -> 117 us  [group_move(): return lax.ppermute(values, 'tensor', moves)]
  transfers between devices with their start and end apart: 37 -> 52, of which waited for: 21 -> 20; matrix products, arithmetic and copies ran while one was open for 16% -> 28% of each run, Pallas kernels for 7% -> 10%
where the time goes in v3:
time: 551 us; the launch traced here: 540 us
  waiting for transfers between devices  226 us (41%)
  matrix products  97.1 us (18%)
  other arithmetic  56.2 us (10%)
  Pallas kernels  52.8 us (10%)
  starting transfers between devices  44.8 us (8%)
  local copies, waits for them, and re-layouts  39.8 us (7%)
  between operations  16 us (3%)
  blocking collectives  7.2 us (1%)
    ppermute x11, waiting for transfers between devices, group_move(): return lax.ppermute(values, 'tensor', moves)  117 us
    ppermute x27, waiting for transfers between devices, dp_move(): return lax.ppermute(values, 'dp', [(i, i ^ bit) for i in range(dp_size)])  96 us
    dot_general x18, matrix products, contract(): lax.dot_general(left, right, (((left_dim,), (right_dim,)), ((), ())), pre...  71 us
    pallas_call x2, Pallas kernels, attend_back(): pl.pallas_call(attend_back_kernel, grid=(blocks,), in_specs=[column_spec(...  32 us
    ppermute x27, starting transfers between devices, dp_move(): return lax.ppermute(values, 'dp', [(i, i ^ bit) for i in range(dp_size)])  25.9 us
    pallas_call x2, Pallas kernels, attend(): pl.pallas_call(attend_kernel, grid=(blocks,), in_specs=[column_spec(3 * L...  20.8 us
    unnamed x141, local copies, waits for them, and re-layouts  16 us
    ppermute x11, starting transfers between devices, group_move(): return lax.ppermute(values, 'tensor', moves)  14.5 us
  transfers between devices with their start and end apart: 52, of which 20 were waited for; matrix products, arithmetic and copies ran while one was open for 28% of the time, Pallas kernels for 10%

profile of v3, /device:TPU:0, one launch (start us, length us, event | category | flops | bytes accessed | tf_op | source)
XLA Modules:
  0.0 540.1 jit_solution(3825496862791197064)
XLA Ops:
  18.3 7.2 %all_gather.6 = bf16[2,6144]{1,0:T(2,128)(2,1)S(1)} all-gather(bf16[2,1536]{1,0:T(2,128)(2,1)S(1)} %fusion.20), channel_id=1, replica_groups=mesh['dp'=8,'tensor'=4] {'tensor'}, dimensions={1}, use_global_device_ids=true | all-gather | bytes 30720 | tf_op jit(solution)/shard_map/all_gather | solution.py:286
  40.4 10.2 %attend.2 = (bf16[1024,256]{1,0:T(8,128)(2,1)}, f32[2,2,1024]{2,1,0:T(2,128)}) custom-call(bf16[1024,768]{1,0:T(8,128)(2,1)} %add_convert_fusion.4.qkv_ref), custom_call_target="tpu_custom_call" | custom-call | tf_op jit(solution)/shard_map/attend/pallas_call | solution.py:125
  50.7 26.7 %collective-permute-done.4 = bf16[1536]{0:T(1024)(128)(2,1)S(1)} collective-permute-done((bf16[1536]{0:T(1024)(128)(2,1)S(1)}, bf16[1536]{0:T(1024)(128)(2,1)S(1)}, u32[]{:S(2)}, u32[]{:S(2)}) %collective-permute-start.4) | collective-permute-done | bytes 3104 | tf_op jit(solution)/shard_map/ppermute | solution.py:185
  77.4 5.0 add_convert_fusion.3.qkv_ref
  82.5 10.6 %attend.3 = (bf16[1024,256]{1,0:T(8,128)(2,1)}, f32[2,2,1024]{2,1,0:T(2,128)}) custom-call(bf16[1024,768]{1,0:T(8,128)(2,1)} %add_convert_fusion.3.qkv_ref), custom_call_target="tpu_custom_call" | custom-call | tf_op jit(solution)/shard_map/attend/pallas_call | solution.py:125
  93.1 10.2 %all-gather.2.cloned.1.call-done = bf16[1024,2048]{1,0:T(8,128)(2,1)} async-done(((bf16[128,2048]{1,0:T(8,128)(2,1)}), bf16[1024,2048]{1,0:T(8,128)(2,1)}) %all-gather.2.cloned.1.call-update) | async-done | bytes 4194320 | tf_op jit(solution)/shard_map/all_gather | solution.py:219
  114.7 5.0 fusion.40
  119.7 6.3 %convert_reduce_fusion = (f32[1024]{0:T(1024)S(1)}, bf16[1024,1024]{1,0:T(8,128)(2,1)S(1)}) fusion(f32[1024,1024]{1,0:T(8,128)S(1)} %fusion.40, f32[1024]{0:T(1024)S(1)} %slice_convert_fusion.4, bf16[1024,2048]{1,0:T(8,128)(2,1)S(1)} %copy-done.62, bf16[512,1024]{1,0:T(8,128)(2,1)} %collective-permute-done.8, bf16[512,1024]{1,0:T(8,128)(2,1)} %get-tuple-element.125), kind=kOutput, calls=%fused_computation.20 | convolution fusion | flops 2175794176 | bytes 10493952 | tf_op jit(solution)/shard_map/dot_general | solution.py:40
  128.4 4.3 fusion.75
  132.7 4.8 fusion.77
  137.5 6.4 %convert_reduce_fusion.1 = (f32[1024]{0:T(1024)S(1)}, bf16[1024,1024]{1,0:T(8,128)(2,1)S(1)}) fusion(f32[1024,1024]{1,0:T(8,128)S(1)} %fusion.75, f32[1024]{0:T(1024)S(1)} %convert_element_type.302, bf16[1024,1024]{1,0:T(8,128)(2,1)S(1)} %copy-done.53, bf16[512,1024]{1,0:T(8,128)(2,1)} %collective-permute-done.8, bf16[512,1024]{1,0:T(8,128)(2,1)} %get-tuple-element.125), kind=kOutput, calls=%fused_computation.21 | convolution fusion | flops 2175794176 | bytes 10493952 | tf_op jit(solution)/shard_map/dot_general | solution.py:40
  146.6 5.3 convolution_add_fusion.4
  152.5 5.9 %convolution_convert_fusion.1 = bf16[1024,1024]{1,0:T(8,128)(2,1)} fusion(bf16[512,1024]{1,0:T(8,128)(2,1)} %collective-permute-done.8, bf16[512,1024]{1,0:T(8,128)(2,1)} %get-tuple-element.125, f32[1024,1024]{1,0:T(8,128)S(1)} %fusion.40, f32[1024]{0:T(1024)S(1)} %slice_convert_fusion.4), kind=kOutput, calls=%fused_computation.85 | convolution fusion | flops 2163212288 | bytes 8392704 | tf_op jit(solution)/shard_map/dot_general | solution.py:40
  159.9 5.2 convolution_convert_fusion
  171.0 6.6 %fusion.72 = f32[1024,1024]{1,0:T(8,128)} fusion(bf16[512,1024]{1,0:T(8,128)(2,1)} %collective-permute-done.8, bf16[512,1024]{1,0:T(8,128)(2,1)} %get-tuple-element.125, f32[1024,1024]{1,0:T(8,128)S(1)} %fusion.75, f32[1024]{0:T(1024)S(1)} %convert_element_type.302), kind=kOutput, calls=%fused_computation.244 | convolution fusion | flops 2162163712 | bytes 10489856 | tf_op jit(solution)/shard_map/dot_general | solution.py:40
  179.0 3.9 fusion.74
  183.0 68.5 %collective-permute-done.23 = f32[2,1024]{1,0:T(2,128)S(1)} collective-permute-done((f32[2,1024]{1,0:T(2,128)S(1)}, f32[2,1024]{1,0:T(2,128)S(1)}, u32[]{:S(2)}, u32[]{:S(2)}) %collective-permute-start.23) | collective-permute-done | bytes 8224 | tf_op jit(solution)/shard_map/ppermute | solution.py:185
  257.2 16.1 %attend_back.2 = bf16[1024,768]{1,0:T(8,128)(2,1)} custom-call(bf16[1024,768]{1,0:T(8,128)(2,1)} %add_convert_fusion.3.qkv_ref, bf16[1024,256]{1,0:T(8,128)(2,1)} %convolution_convert_fusion.5.do_ref, f32[2,2,1024]{2,1,0:T(2,128)} %get-tuple-element.48.lse_ref), custom_call_target="tpu_custom_call" | custom-call | tf_op jit(solution)/shard_map/attend_back/pallas_call | solution.py:141
  276.3 16.0 %attend_back.3 = bf16[1024,768]{1,0:T(8,128)(2,1)} custom-call(bf16[1024,768]{1,0:T(8,128)(2,1)} %add_convert_fusion.4.qkv_ref, bf16[1024,256]{1,0:T(8,128)(2,1)} %convolution_convert_fusion.4.do_ref, f32[2,2,1024]{2,1,0:T(2,128)} %get-tuple-element.50.lse_ref), custom_call_target="tpu_custom_call" | custom-call | tf_op jit(solution)/shard_map/attend_back/pallas_call | solution.py:141
  309.3 5.2 convolution_add_fusion.2
  320.6 21.8 %collective-permute-done.21 = f32[1536]{0:T(1024)S(1)} collective-permute-done((f32[1536]{0:T(1024)S(1)}, f32[1536]{0:T(1024)S(1)}, u32[]{:S(2)}, u32[]{:S(2)}) %collective-permute-start.21) | collective-permute-done | bytes 6176 | tf_op jit(solution)/shard_map/ppermute | solution.py:185
  351.0 16.5 %collective-permute-done.46 = bf16[256,1024]{1,0:T(8,128)(2,1)S(1)} collective-permute-done((bf16[256,1024]{1,0:T(8,128)(2,1)S(1)}, bf16[256,1024]{1,0:T(8,128)(2,1)S(1)}, u32[]{:S(2)}, u32[]{:S(2)}) %collective-permute-start.46) | collective-permute-done | bytes 524320 | tf_op jit(solution)/shard_map/ppermute | solution.py:231
  375.5 4.7 collective-permute-done.40
  398.5 8.6 %collective-permute-done.26 = bf16[8,4352]{1,0:T(8,128)(2,1)S(1)} collective-permute-done((bf16[8,4352]{1,0:T(8,128)(2,1)S(1)}, bf16[8,4352]{1,0:T(8,128)(2,1)S(1)}, u32[]{:S(2)}, u32[]{:S(2)}) %collective-permute-start.26) | collective-permute-done | bytes 69664 | tf_op jit(solution)/shard_map/ppermute | solution.py:231
  421.0 5.5 %collective-permute-done.48 = bf16[128,1024]{1,0:T(8,128)(2,1)} collective-permute-done((bf16[128,1024]{1,0:T(8,128)(2,1)S(1)}, bf16[128,1024]{1,0:T(8,128)(2,1)}, u32[]{:S(2)}, u32[]{:S(2)}) %collective-permute-start.48) | collective-permute-done | bytes 262176 | tf_op jit(solution)/shard_map/ppermute | solution.py:231
  435.2 28.1 %collective-permute-done.34 = bf16[256,512]{1,0:T(8,128)(2,1)S(1)} collective-permute-done((bf16[256,512]{1,0:T(8,128)(2,1)S(1)}, bf16[256,512]{1,0:T(8,128)(2,1)S(1)}, u32[]{:S(2)}, u32[]{:S(2)}) %collective-permute-start.34) | collective-permute-done | bytes 262176 | tf_op jit(solution)/shard_map/ppermute | solution.py:231
  463.9 5.4 %collective-permute-done.35 = bf16[128,512]{1,0:T(8,128)(2,1)S(1)} collective-permute-done((bf16[128,512]{1,0:T(8,128)(2,1)S(1)}, bf16[128,512]{1,0:T(8,128)(2,1)S(1)}, u32[]{:S(2)}, u32[]{:S(2)}) %collective-permute-start.35) | collective-permute-done | bytes 131104 | tf_op jit(solution)/shard_map/ppermute | solution.py:231
  482.2 5.6 %collective-permute-done.37 = bf16[256,512]{1,0:T(8,128)(2,1)S(1)} collective-permute-done((bf16[256,512]{1,0:T(8,128)(2,1)S(1)}, bf16[256,512]{1,0:T(8,128)(2,1)S(1)}, u32[]{:S(2)}, u32[]{:S(2)}) %collective-permute-start.37) | collective-permute-done | bytes 262176 | tf_op jit(solution)/shard_map/ppermute | solution.py:231
  488.3 5.1 collective-permute-done.31
  495.8 8.8 %collective-permute-done.38 = bf16[512,512]{1,0:T(8,128)(2,1)S(1)} collective-permute-done((bf16[512,512]{1,0:T(8,128)(2,1)S(1)}, bf16[512,512]{1,0:T(8,128)(2,1)S(1)}, u32[]{:S(2)}, u32[]{:S(2)}) %collective-permute-start.38) | collective-permute-done | bytes 524320 | tf_op jit(solution)/shard_map/ppermute | solution.py:231
  512.6 3.8 copy.48
  516.5 4.0 copy.49
  (374 shorter events, 176.8 us)
Async XLA Ops:
  7.2 96.1 %all-gather.2.cloned.1.call-start = ((), (), s32[]{:S(2)}) async-start(), calls=%async_computation | async-start | bytes 4718592 | tf_op jit(solution)/shard_map/all_gather | solution.py:219
  9.3 19.5 %collective-permute-start = (bf16[128,2048]{1,0:T(8,128)(2,1)}, bf16[128,2048]{1,0:T(8,128)(2,1)}, u32[]{:S(2)}, u32[]{:S(2)}) collective-permute-start(bf16[128,2048]{1,0:T(8,128)(2,1)} %pad_maximum_fusion.8), channel_id=1, source_target_pairs={{0,2},{1,3},{2,0},{3,1},{4,6},{5,7},{6,4},{7,5},{8,10},{9,11},{10,... | collective-permute-start | bytes 1572872 | tf_op jit(solution)/shard_map/ppermute | solution.py:185
  29.3 48.1 %collective-permute-start.2 = (bf16[1024,768]{0,1:T(8,128)(2,1)}, bf16[1024,768]{0,1:T(8,128)(2,1)}, u32[]{:S(2)}, u32[]{:S(2)}) collective-permute-start(bf16[1024,768]{0,1:T(8,128)(2,1)} %bitcast.76), channel_id=1, source_target_pairs={{0,2},{1,3},{2,0},{3,1},{4,6},{5,7},{6,4},{7,5},{8,10},{9,11},{10,... | collective-permute-start | bytes 4718600 | tf_op jit(solution)/shard_map/ppermute | solution.py:185
  31.0 46.3 %collective-permute-start.3 = (bf16[256,1024]{1,0:T(8,128)(2,1)}, bf16[256,1024]{1,0:T(8,128)(2,1)}, u32[]{:S(2)}, u32[]{:S(2)}) collective-permute-start(bf16[256,1024]{1,0:T(8,128)(2,1)} %param.19), channel_id=1, source_target_pairs={{0,2},{1,3},{2,0},{3,1},{4,6},{5,7},{6,4},{7,5},{8,10},{9,11},{10,... | collective-permute-start | bytes 1572872 | tf_op jit(solution)/shard_map/ppermute | solution.py:185
  31.3 46.0 %collective-permute-start.4 = (bf16[1536]{0:T(1024)(128)(2,1)S(1)}, bf16[1536]{0:T(1024)(128)(2,1)S(1)}, u32[]{:S(2)}, u32[]{:S(2)}) collective-permute-start(bf16[1536]{0:T(1024)(128)(2,1)S(1)} %pad_maximum_fusion.27), channel_id=1, source_target_pairs={{0,2},{1,3},{2,0},{3,1},{4,6},{5,7},{6,4},{7,5},{8,10},{9,11},{10,... | collective-permute-start | bytes 9224 | tf_op jit(solution)/shard_map/ppermute | solution.py:185
  146.5 19.3 %collective-permute-start.9 = (bf16[512,1024]{1,0:T(8,128)(2,1)S(1)}, bf16[512,1024]{1,0:T(8,128)(2,1)S(1)}, u32[]{:S(2)}, u32[]{:S(2)}) collective-permute-start(bf16[512,1024]{1,0:T(8,128)(2,1)S(1)} %slice.257), channel_id=1, source_target_pairs={{0,1},{1,0},{2,3},{3,2},{4,5},{5,4},{6,7},{7,6},{8,9},{9,8},{10,11... | collective-permute-start | bytes 3145736 | tf_op jit(solution)/shard_map/ppermute | solution.py:181
  152.0 14.8 %collective-permute-start.7 = (bf16[512,1024]{1,0:T(8,128)(2,1)S(1)}, bf16[512,1024]{1,0:T(8,128)(2,1)S(1)}, u32[]{:S(2)}, u32[]{:S(2)}) collective-permute-start(bf16[512,1024]{1,0:T(8,128)(2,1)S(1)} %slice.258), channel_id=1, source_target_pairs={{0,1},{1,0},{2,3},{3,2},{4,5},{5,4},{6,7},{7,6},{8,9},{9,8},{10,11... | collective-permute-start | bytes 3145736 | tf_op jit(solution)/shard_map/ppermute | solution.py:181
  158.5 133.8 %collective-permute-start.11 = (bf16[1024,1024]{1,0:T(8,128)(2,1)}, bf16[1024,1024]{1,0:T(8,128)(2,1)}, u32[]{:S(2)}, u32[]{:S(2)}) collective-permute-start(bf16[1024,1024]{1,0:T(8,128)(2,1)} %convolution_convert_fusion.1), channel_id=1, source_target_pairs={{0,2},{1,3},{2,0},{3,1},{4,6},{5,7},{6,4},{7,5},{8,10},{9,11},{10,... | collective-permute-start | bytes 6291464 | tf_op jit(solution)/shard_map/ppermute | solution.py:185
  165.2 137.1 %collective-permute-start.12 = (bf16[1024,1024]{1,0:T(8,128)(2,1)}, bf16[1024,1024]{1,0:T(8,128)(2,1)}, u32[]{:S(2)}, u32[]{:S(2)}) collective-permute-start(bf16[1024,1024]{1,0:T(8,128)(2,1)} %convolution_convert_fusion), channel_id=1, source_target_pairs={{0,2},{1,3},{2,0},{3,1},{4,6},{5,7},{6,4},{7,5},{8,10},{9,11},{10,... | collective-permute-start | bytes 6291464 | tf_op jit(solution)/shard_map/ppermute | solution.py:185
  170.3 81.1 %collective-permute-start.10 = (bf16[512,1024]{1,0:T(8,128)(2,1)S(1)}, bf16[512,1024]{1,0:T(8,128)(2,1)S(1)}, u32[]{:S(2)}, u32[]{:S(2)}) collective-permute-start(bf16[512,1024]{1,0:T(8,128)(2,1)S(1)} %get-tuple-element.131), channel_id=1, source_target_pairs={{0,1},{1,0},{2,3},{3,2},{4,5},{5,4},{6,7},{7,6},{8,9},{9,8},{10,11... | collective-permute-start | bytes 3145736 | tf_op jit(solution)/shard_map/ppermute | solution.py:181
  177.6 73.8 %collective-permute-start.23 = (f32[2,1024]{1,0:T(2,128)S(1)}, f32[2,1024]{1,0:T(2,128)S(1)}, u32[]{:S(2)}, u32[]{:S(2)}) collective-permute-start(f32[2,1024]{1,0:T(2,128)S(1)} %fusion.70), channel_id=1, source_target_pairs={{0,2},{1,3},{2,0},{3,1},{4,6},{5,7},{6,4},{7,5},{8,10},{9,11},{10,... | collective-permute-start | bytes 24584 | tf_op jit(solution)/shard_map/ppermute | solution.py:185
  253.1 116.6 %collective-permute-start.15 = (bf16[1024,256]{1,0:T(8,128)(2,1)}, bf16[1024,256]{1,0:T(8,128)(2,1)}, u32[]{:S(2)}, u32[]{:S(2)}) collective-permute-start(bf16[1024,256]{1,0:T(8,128)(2,1)} %convolution_convert_fusion.3), channel_id=1, source_target_pairs={{0,2},{1,3},{2,0},{3,1},{4,6},{5,7},{6,4},{7,5},{8,10},{9,11},{10,... | collective-permute-start | bytes 1572872 | tf_op jit(solution)/shard_map/ppermute | solution.py:185
  297.1 45.5 %collective-permute-start.45 = (bf16[512,1024]{1,0:T(8,128)(2,1)}, bf16[512,1024]{1,0:T(8,128)(2,1)}, u32[]{:S(2)}, u32[]{:S(2)}) collective-permute-start(bf16[512,1024]{1,0:T(8,128)(2,1)} %constant_dynamic-slice_fusion.2), channel_id=1, source_target_pairs={{0,4},{4,0},{8,12},{12,8},{16,20},{20,16},{24,28},{28,24},{1,5},{5... | collective-permute-start | bytes 3145736 | tf_op jit(solution)/shard_map/ppermute | solution.py:231
  305.8 39.8 %collective-permute-start.39 = (bf16[512,1024]{1,0:T(8,128)(2,1)}, bf16[512,1024]{1,0:T(8,128)(2,1)}, u32[]{:S(2)}, u32[]{:S(2)}) collective-permute-start(bf16[512,1024]{1,0:T(8,128)(2,1)} %constant_dynamic-slice_fusion.5), channel_id=1, source_target_pairs={{0,8},{4,12},{8,0},{12,4},{16,24},{20,28},{24,16},{28,20},{1,9},{5... | collective-permute-start | bytes 3145736 | tf_op jit(solution)/shard_map/ppermute | solution.py:231
  307.0 62.7 %collective-permute-start.14 = (bf16[1024,768]{1,0:T(8,128)(2,1)}, bf16[1024,768]{1,0:T(8,128)(2,1)}, u32[]{:S(2)}, u32[]{:S(2)}) collective-permute-start(bf16[1024,768]{1,0:T(8,128)(2,1)} %convolution_convert_fusion.2), channel_id=1, source_target_pairs={{0,2},{1,3},{2,0},{3,1},{4,6},{5,7},{6,4},{7,5},{8,10},{9,11},{10,... | collective-permute-start | bytes 4718600 | tf_op jit(solution)/shard_map/ppermute | solution.py:185
  316.3 26.1 %collective-permute-start.21 = (f32[1536]{0:T(1024)S(1)}, f32[1536]{0:T(1024)S(1)}, u32[]{:S(2)}, u32[]{:S(2)}) collective-permute-start(f32[1536]{0:T(1024)S(1)} %pad_maximum_fusion.24), channel_id=1, source_target_pairs={{0,2},{1,3},{2,0},{3,1},{4,6},{5,7},{6,4},{7,5},{8,10},{9,11},{10,... | collective-permute-start | bytes 18440 | tf_op jit(solution)/shard_map/ppermute | solution.py:185
  344.7 22.9 %collective-permute-start.46 = (bf16[256,1024]{1,0:T(8,128)(2,1)S(1)}, bf16[256,1024]{1,0:T(8,128)(2,1)S(1)}, u32[]{:S(2)}, u32[]{:S(2)}) collective-permute-start(bf16[256,1024]{1,0:T(8,128)(2,1)S(1)} %constant_dynamic-slice_fusion.1), channel_id=1, source_target_pairs={{0,8},{4,12},{8,0},{12,4},{16,24},{20,28},{24,16},{28,20},{1,9},{5... | collective-permute-start | bytes 1572872 | tf_op jit(solution)/shard_map/ppermute | solution.py:231
  347.6 32.7 %collective-permute-start.40 = (bf16[256,1024]{1,0:T(8,128)(2,1)S(1)}, bf16[256,1024]{1,0:T(8,128)(2,1)S(1)}, u32[]{:S(2)}, u32[]{:S(2)}) collective-permute-start(bf16[256,1024]{1,0:T(8,128)(2,1)S(1)} %constant_dynamic-slice_fusion.4), channel_id=1, source_target_pairs={{0,16},{4,20},{8,24},{12,28},{16,0},{20,4},{24,8},{28,12},{1,17},{... | collective-permute-start | bytes 1572872 | tf_op jit(solution)/shard_map/ppermute | solution.py:231
  369.3 42.2 %collective-permute-start.47 = (bf16[128,1024]{1,0:T(8,128)(2,1)}, bf16[128,1024]{1,0:T(8,128)(2,1)}, u32[]{:S(2)}, u32[]{:S(2)}) collective-permute-start(bf16[128,1024]{1,0:T(8,128)(2,1)} %constant_dynamic-slice_fusion), channel_id=1, source_target_pairs={{0,16},{4,20},{8,24},{12,28},{16,0},{20,4},{24,8},{28,12},{1,17},{... | collective-permute-start | bytes 786440 | tf_op jit(solution)/shard_map/ppermute | solution.py:231
  382.2 36.8 %collective-permute-start.41 = (bf16[128,1024]{1,0:T(8,128)(2,1)}, bf16[128,1024]{1,0:T(8,128)(2,1)}, u32[]{:S(2)}, u32[]{:S(2)}) collective-permute-start(bf16[128,1024]{1,0:T(8,128)(2,1)} %constant_dynamic-slice_fusion.3), channel_id=1, source_target_pairs={{0,4},{4,0},{8,12},{12,8},{16,20},{20,16},{24,28},{28,24},{1,5},{5... | collective-permute-start | bytes 786440 | tf_op jit(solution)/shard_map/ppermute | solution.py:231
  393.0 37.1 %collective-permute-start.33 = (bf16[512,512]{1,0:T(8,128)(2,1)}, bf16[512,512]{1,0:T(8,128)(2,1)}, u32[]{:S(2)}, u32[]{:S(2)}) collective-permute-start(bf16[512,512]{1,0:T(8,128)(2,1)} %fusion.45), channel_id=1, source_target_pairs={{0,8},{4,12},{8,0},{12,4},{16,24},{20,28},{24,16},{28,20},{1,9},{5... | collective-permute-start | bytes 1572872 | tf_op jit(solution)/shard_map/ppermute | solution.py:231
  397.0 34.9 %collective-permute-start.27 = (bf16[512,512]{1,0:T(8,128)(2,1)}, bf16[512,512]{1,0:T(8,128)(2,1)}, u32[]{:S(2)}, u32[]{:S(2)}) collective-permute-start(bf16[512,512]{1,0:T(8,128)(2,1)} %constant_dynamic-slice_fusion.10), channel_id=1, source_target_pairs={{0,4},{4,0},{8,12},{12,8},{16,20},{20,16},{24,28},{28,24},{1,5},{5... | collective-permute-start | bytes 1572872 | tf_op jit(solution)/shard_map/ppermute | solution.py:231
  412.5 13.9 %collective-permute-start.48 = (bf16[128,1024]{1,0:T(8,128)(2,1)S(1)}, bf16[128,1024]{1,0:T(8,128)(2,1)}, u32[]{:S(2)}, u32[]{:S(2)}) collective-permute-start(bf16[128,1024]{1,0:T(8,128)(2,1)S(1)} %add_convert_fusion.13), channel_id=1, source_target_pairs={{0,16},{4,20},{8,24},{12,28},{16,0},{20,4},{24,8},{28,12},{1,17},{... | collective-permute-start | bytes 786440 | tf_op jit(solution)/shard_map/ppermute | solution.py:231
  427.5 44.2 %collective-permute-start.49 = (bf16[256,1024]{1,0:T(8,128)(2,1)S(1)}, bf16[256,1024]{1,0:T(8,128)(2,1)S(1)}, u32[]{:S(2)}, u32[]{:S(2)}) collective-permute-start(bf16[256,1024]{1,0:T(8,128)(2,1)S(1)} %pad_maximum_fusion.12), channel_id=1, source_target_pairs={{0,8},{4,12},{8,0},{12,4},{16,24},{20,28},{24,16},{28,20},{1,9},{5... | collective-permute-start | bytes 1572872 | tf_op jit(solution)/shard_map/ppermute | solution.py:231
  427.6 60.3 %collective-permute-start.43 = (bf16[256,1024]{1,0:T(8,128)(2,1)S(1)}, bf16[256,1024]{1,0:T(8,128)(2,1)S(1)}, u32[]{:S(2)}, u32[]{:S(2)}) collective-permute-start(bf16[256,1024]{1,0:T(8,128)(2,1)S(1)} %pad_maximum_fusion.11), channel_id=1, source_target_pairs={{0,16},{4,20},{8,24},{12,28},{16,0},{20,4},{24,8},{28,12},{1,17},{... | collective-permute-start | bytes 1572872 | tf_op jit(solution)/shard_map/ppermute | solution.py:231
  431.4 32.0 %collective-permute-start.34 = (bf16[256,512]{1,0:T(8,128)(2,1)S(1)}, bf16[256,512]{1,0:T(8,128)(2,1)S(1)}, u32[]{:S(2)}, u32[]{:S(2)}) collective-permute-start(bf16[256,512]{1,0:T(8,128)(2,1)S(1)} %constant_dynamic-slice_fusion.7), channel_id=1, source_target_pairs={{0,16},{4,20},{8,24},{12,28},{16,0},{20,4},{24,8},{28,12},{1,17},{... | collective-permute-start | bytes 786440 | tf_op jit(solution)/shard_map/ppermute | solution.py:231
  433.2 30.6 %collective-permute-start.28 = (bf16[256,512]{1,0:T(8,128)(2,1)S(1)}, bf16[256,512]{1,0:T(8,128)(2,1)S(1)}, u32[]{:S(2)}, u32[]{:S(2)}) collective-permute-start(bf16[256,512]{1,0:T(8,128)(2,1)S(1)} %constant_dynamic-slice_fusion.9), channel_id=1, source_target_pairs={{0,8},{4,12},{8,0},{12,4},{16,24},{20,28},{24,16},{28,20},{1,9},{5... | collective-permute-start | bytes 786440 | tf_op jit(solution)/shard_map/ppermute | solution.py:231
  473.1 50.9 %collective-permute-start.50 = (bf16[512,1024]{1,0:T(8,128)(2,1)}, bf16[512,1024]{1,0:T(8,128)(2,1)}, u32[]{:S(2)}, u32[]{:S(2)}) collective-permute-start(bf16[512,1024]{1,0:T(8,128)(2,1)} %pad_maximum_fusion.6), channel_id=1, source_target_pairs={{0,4},{4,0},{8,12},{12,8},{16,20},{20,16},{24,28},{28,24},{1,5},{5... | collective-permute-start | bytes 3145736 | tf_op jit(solution)/shard_map/ppermute | solution.py:231
  475.9 11.9 %collective-permute-start.37 = (bf16[256,512]{1,0:T(8,128)(2,1)S(1)}, bf16[256,512]{1,0:T(8,128)(2,1)S(1)}, u32[]{:S(2)}, u32[]{:S(2)}) collective-permute-start(bf16[256,512]{1,0:T(8,128)(2,1)S(1)} %pad_maximum_fusion.14), channel_id=1, source_target_pairs={{0,16},{4,20},{8,24},{12,28},{16,0},{20,4},{24,8},{28,12},{1,17},{... | collective-permute-start | bytes 786440 | tf_op jit(solution)/shard_map/ppermute | solution.py:231
  487.9 16.7 %collective-permute-start.38 = (bf16[512,512]{1,0:T(8,128)(2,1)S(1)}, bf16[512,512]{1,0:T(8,128)(2,1)S(1)}, u32[]{:S(2)}, u32[]{:S(2)}) collective-permute-start(bf16[512,512]{1,0:T(8,128)(2,1)S(1)} %pad_maximum_fusion.10), channel_id=1, source_target_pairs={{0,8},{4,12},{8,0},{12,4},{16,24},{20,28},{24,16},{28,20},{1,9},{5... | collective-permute-start | bytes 1572872 | tf_op jit(solution)/shard_map/ppermute | solution.py:231
  494.4 15.0 %collective-permute-start.32 = (bf16[512,512]{1,0:T(8,128)(2,1)}, bf16[512,512]{1,0:T(8,128)(2,1)}, u32[]{:S(2)}, u32[]{:S(2)}) collective-permute-start(bf16[512,512]{1,0:T(8,128)(2,1)} %pad_maximum_fusion.9), channel_id=1, source_target_pairs={{0,4},{4,0},{8,12},{12,8},{16,20},{20,16},{24,28},{28,24},{1,5},{5... | collective-permute-start | bytes 1572872 | tf_op jit(solution)/shard_map/ppermute | solution.py:231
  495.7 32.8 %collective-permute-start.44 = (bf16[512,1024]{1,0:T(8,128)(2,1)}, bf16[512,1024]{1,0:T(8,128)(2,1)}, u32[]{:S(2)}, u32[]{:S(2)}) collective-permute-start(bf16[512,1024]{1,0:T(8,128)(2,1)} %pad_maximum_fusion.5), channel_id=1, source_target_pairs={{0,8},{4,12},{8,0},{12,4},{16,24},{20,28},{24,16},{28,20},{1,9},{5... | collective-permute-start | bytes 3145736 | tf_op jit(solution)/shard_map/ppermute | solution.py:231
  (85 other events, 619.8 us)
Sparse Core Ops, SparseCore 0:
  29.0 74.2 all-gather.1
